TPU v7x, 128 devices: a whole 4x4x4 slice. The times are simulated.
128 devices in a mesh: row: 8 (over z, core), col: 16 (over y, x).
Axes of the slice: x: 4, y: 4, z: 4, core: 2. Of those that a mesh axis runs over, the one named last changes fastest.
Arguments:
- initial: bfloat16 [8, 24576], P(None, ('row', 'col')), may hold values from -8 to 8
- matrix: bfloat16 [24576, 24576], P('row', 'col'), may hold values from -1 to 4, as said below
Outputs:
- vectors: float32 [8, 24576], P(None, ('row', 'col'))
- estimates: float32 [4, 8], replicated
Inputs may be any that keep to these rules, and one draw needn't show every extreme that they name: matrix is symmetric: entry (i, j) equals entry (j, i).
All inputs are finite; a program needn't handle non-finite values.
Results may differ from a plain program's by a relative error of at most 0.008.
Values may be sent and summed in bfloat16 or wider, within the bound.
No kernel may reach another device: no remote copies, remote signals or barrier semaphores. Data moves between devices by JAX's collectives and lax.ppermute only.
A program may use at most 64 MiB of HBM per device.

v0:
```python
import jax
import jax.numpy as jnp
from jax import lax
from jax.sharding import PartitionSpec as P

ITERS = 4


def copy_for_each(value, axis):
    copies = jnp.broadcast_to(value, (lax.axis_size(axis), *value.shape))
    return lax.all_to_all(copies, axis, split_axis=0, concat_axis=0, tiled=True)


def joined_along(pieces, dim):
    dims = list(pieces.shape[1:])
    dims[dim] *= pieces.shape[0]
    return jnp.moveaxis(pieces, 0, dim).reshape(dims)


def gathered_copies(value, axis, dim):
    pieces = copy_for_each(value, axis)
    return joined_along(pieces, dim)


def over_copies(value, axis):
    everything = copy_for_each(value, axis)
    return jnp.sum(everything, axis=0)


def normalise(summed, gram_matrix):
    factor = jnp.linalg.cholesky(gram_matrix)
    updated = jax.scipy.linalg.solve_triangular(factor, summed, lower=True)
    return (updated, jnp.diagonal(factor))


def local_gram(summed):
    return jnp.dot(summed, summed.T, precision=lax.Precision.HIGHEST)


def shards(initial, matrix):
    diagonals = []
    current = gathered_copies(initial, "col", 1)
    updated = current.astype(jnp.float32)
    for iteration in range(ITERS):
        if iteration % 2 == 0:
            partial_sum = jnp.dot(current, matrix, preferred_element_type=jnp.float32)
            summed = over_copies(partial_sum, "row")
            gram_matrix = over_copies(local_gram(summed), "col")
        else:
            partial_sum = lax.dot_general(
                current, matrix, (((1,), (1,)), ((), ())), preferred_element_type=jnp.float32
            )
            summed = over_copies(partial_sum, "col")
            gram_matrix = over_copies(local_gram(summed), "row")
        updated, diagonal = normalise(summed, gram_matrix)
        diagonals.append(diagonal)
        current = updated.astype(jnp.bfloat16)
    columns = updated.shape[1] // lax.axis_size("col")
    result = lax.dynamic_slice_in_dim(updated, lax.axis_index("col") * columns, columns, 1)
    return (result, jnp.stack(diagonals))


def solution(mesh):
    return jax.shard_map(
        shards,
        mesh=mesh,
        in_specs=(P(None, ("row", "col")), P("row", "col")),
        out_specs=(P(None, ("row", "col")), P()),
        check_vma=False,
    )
```

profile of v0, /device:TPU:0, one launch (start us, length us, event | category | flops | bytes accessed | tf_op | source)
XLA Modules:
  0.0 168.4 jit_solution(4725991481218492036)
XLA Ops:
  0.6 0.7 broadcast_in_dim.38
  1.3 14.6 %all_to_all.45 = bf16[16,8,192]{2,1,0:T(8,128)(2,1)S(1)} all-to-all(bf16[16,8,192]{2,1,0:T(8,128)(2,1)S(1)} %broadcast_in_dim.38), channel_id=1, replica_groups=mesh['row'=8,'col'=16] {'col'}, dimensions={0} | all-to-all | bytes 98304 | tf_op jit(solution)/shard_map/all_to_all | solution.py:11
  16.0 5.0 %fusion.29 = f32[8,1536]{1,0:T(8,128)S(1)} fusion(bf16[8,3072]{1,0:T(8,128)(2,1)S(1)} %reshape.18, bf16[3072,1536]{1,0:T(8,128)(2,1)} %param.8), kind=kOutput, calls=%fused_computation.47 | convolution fusion | flops 75497472 | bytes 9535488 | tf_op jit(solution)/shard_map/dot_general | solution.py:46
  21.1 14.1 %all_to_all.46 = f32[8,8,1536]{2,1,0:T(8,128)S(1)} all-to-all(f32[8,8,1536]{2,1,0:T(8,128)S(1)} %broadcast_in_dim.39), channel_id=1, replica_groups=mesh['row'=8,'col'=16] {'row'}, dimensions={0} | all-to-all | bytes 786432 | tf_op jit(solution)/shard_map/all_to_all | solution.py:11
  35.2 0.2 fusion.30
  35.4 10.8 %all_to_all.47 = f32[16,8,8]{2,1,0:T(8,128)S(1)} all-to-all(f32[16,8,8]{2,1,0:T(8,128)S(1)} %broadcast_in_dim.40), channel_id=1, replica_groups=mesh['row'=8,'col'=16] {'col'}, dimensions={0} | all-to-all | bytes 8192 | tf_op jit(solution)/shard_map/all_to_all | solution.py:11
  46.3 0.7 cholesky.74
  47.0 0.6 compare_reduce_fusion.3
  47.7 0.6 fusion.18
  48.3 0.6 custom-call.18
  49.0 0.2 convolution_convert_fusion.2
  49.2 6.2 %fusion.31 = f32[8,3072]{1,0:T(8,128)S(1)} fusion(bf16[8,1536]{1,0:T(8,128)(2,1)S(1)} %convolution_convert_fusion.2, bf16[3072,1536]{1,0:T(8,128)(2,1)} %param.8), kind=kOutput, calls=%fused_computation.49 | convolution fusion | flops 75497472 | bytes 9560064 | tf_op jit(solution)/shard_map/dot_general | solution.py:50
  55.4 0.2 broadcast_in_dim.41
  55.6 25.4 %all_to_all.48 = f32[16,8,3072]{2,1,0:T(8,128)S(1)} all-to-all(f32[16,8,3072]{2,1,0:T(8,128)S(1)} %broadcast_in_dim.41), channel_id=1, replica_groups=mesh['row'=8,'col'=16] {'col'}, dimensions={0} | all-to-all | bytes 3145728 | tf_op jit(solution)/shard_map/all_to_all | solution.py:11
  81.1 0.3 fusion.32
  81.3 7.9 %all_to_all.49 = f32[8,8,8]{2,1,0:T(8,128)S(1)} all-to-all(f32[8,8,8]{2,1,0:T(8,128)S(1)} %broadcast_in_dim.42), channel_id=1, replica_groups=mesh['row'=8,'col'=16] {'row'}, dimensions={0} | all-to-all | bytes 4096 | tf_op jit(solution)/shard_map/all_to_all | solution.py:11
  89.3 0.7 cholesky.85
  90.1 0.6 compare_reduce_fusion.2
  90.7 0.6 fusion.17
  91.4 0.6 custom-call.19
  92.0 0.3 convolution_convert_fusion
  92.3 5.0 %fusion.33 = f32[8,1536]{1,0:T(8,128)S(1)} fusion(bf16[8,3072]{1,0:T(8,128)(2,1)S(1)} %convolution_convert_fusion, bf16[3072,1536]{1,0:T(8,128)(2,1)} %param.8), kind=kOutput, calls=%fused_computation.51 | convolution fusion | flops 75497472 | bytes 9535488 | tf_op jit(solution)/shard_map/dot_general | solution.py:46
  97.3 11.3 %all_to_all.50 = f32[8,8,1536]{2,1,0:T(8,128)S(1)} all-to-all(f32[8,8,1536]{2,1,0:T(8,128)S(1)} %broadcast_in_dim.43), channel_id=1, replica_groups=mesh['row'=8,'col'=16] {'row'}, dimensions={0} | all-to-all | bytes 786432 | tf_op jit(solution)/shard_map/all_to_all | solution.py:11
  108.7 0.2 fusion.34
  108.9 10.2 %all_to_all.51 = f32[16,8,8]{2,1,0:T(8,128)S(1)} all-to-all(f32[16,8,8]{2,1,0:T(8,128)S(1)} %broadcast_in_dim.44), channel_id=1, replica_groups=mesh['row'=8,'col'=16] {'col'}, dimensions={0} | all-to-all | bytes 8192 | tf_op jit(solution)/shard_map/all_to_all | solution.py:11
  119.2 0.7 cholesky.96
  120.0 0.6 compare_reduce_fusion.1
  120.6 0.6 fusion.16
  121.3 0.6 custom-call.20
  121.9 0.2 convolution_convert_fusion.1
  122.2 6.2 %fusion.35 = f32[8,3072]{1,0:T(8,128)S(1)} fusion(bf16[8,1536]{1,0:T(8,128)(2,1)S(1)} %convolution_convert_fusion.1, bf16[3072,1536]{1,0:T(8,128)(2,1)} %param.8), kind=kOutput, calls=%fused_computation.53 | convolution fusion | flops 75497472 | bytes 9560064 | tf_op jit(solution)/shard_map/dot_general | solution.py:50
  128.4 0.2 broadcast_in_dim.45
  128.5 25.2 %all_to_all.52 = f32[16,8,3072]{2,1,0:T(8,128)S(1)} all-to-all(f32[16,8,3072]{2,1,0:T(8,128)S(1)} %broadcast_in_dim.45), channel_id=1, replica_groups=mesh['row'=8,'col'=16] {'col'}, dimensions={0} | all-to-all | bytes 3145728 | tf_op jit(solution)/shard_map/all_to_all | solution.py:11
  153.8 0.3 fusion.36
  154.1 0.7 broadcast_in_dim.46
  154.7 3.3 %all-to-all-start.8 = ((f32[8,8,8]{2,1,0:T(8,128)}), f32[8,8,8]{2,1,0:T(8,128)S(1)}, u32[]{:S(2)}, u32[]{:S(2)}) async-start(f32[8,8,8]{2,1,0:T(8,128)} %broadcast_in_dim.46), calls=%async_computation.8 | async-start | bytes 65536 | tf_op jit(solution)/shard_map/all_to_all | solution.py:11
  158.1 0.6 gather_fusion
  158.7 0.6 gather_fusion.1
  159.3 0.6 gather_fusion.2
  160.0 3.4 %all-to-all-done.8 = f32[8,8,8]{2,1,0:T(8,128)S(1)} async-done(((f32[8,8,8]{2,1,0:T(8,128)}), f32[8,8,8]{2,1,0:T(8,128)S(1)}, u32[]{:S(2)}, u32[]{:S(2)}) %all-to-all-start.8) | async-done | bytes 2080 | tf_op jit(solution)/shard_map/all_to_all | solution.py:11
  163.5 0.7 cholesky.107
  164.3 0.6 compare_reduce_fusion
  164.9 0.6 select_bitcast_fusion
  165.6 0.6 custom-call.21
  166.2 0.3 fusion
  166.5 0.6 gather_fusion.3
  167.1 0.7 constant_dynamic-slice_fusion
  167.8 0.6 pad_maximum_fusion
  (28 shorter events, 1.1 us)
Async XLA Ops:
  154.7 8.7 %all-to-all-start.8 = ((f32[8,8,8]{2,1,0:T(8,128)}), f32[8,8,8]{2,1,0:T(8,128)S(1)}, u32[]{:S(2)}, u32[]{:S(2)}) async-start(f32[8,8,8]{2,1,0:T(8,128)} %broadcast_in_dim.46), calls=%async_computation.8 | async-start | bytes 65536 | tf_op jit(solution)/shard_map/all_to_all | solution.py:11
where the time goes:
time: 170 us; the launch traced here: 168 us
  blocking collectives  119 us (70%)
  matrix products  24.3 us (14%)
  other arithmetic  11.6 us (7%)
  local copies, waits for them, and re-layouts  5.5 us (3%)
  waiting for transfers between devices  3.44 us (2%)
  starting transfers between devices  3.33 us (2%)
    all_to_all x8, blocking collectives, copy_for_each(): return lax.all_to_all(copies, axis, split_axis=0, concat_axis=0, tiled=True)  119 us
    dot_general x2, matrix products, shards(): lax.dot_general(current, matrix, (((1,), (1,)), ((), ())), preferred_elem...  12.4 us
    dot_general x2, matrix products, shards(): partial_sum = jnp.dot(current, matrix, preferred_element_type=jnp.float32)  9.99 us
    another operation x12, other arithmetic, normalise(): factor = jnp.linalg.cholesky(gram_matrix)  5.57 us
    another operation x8, other arithmetic, normalise(): updated = jax.scipy.linalg.solve_triangular(factor, summed, lower=True)  5.09 us
    all_to_all x1, waiting for transfers between devices, copy_for_each(): return lax.all_to_all(copies, axis, split_axis=0, concat_axis=0, tiled=True)  3.44 us
  transfers between devices with their start and end apart: 1, of which 1 were waited for; matrix products, arithmetic and copies ran while one was open for 1% of the time, Pallas kernels for 0%

commit v1 on v0

v1 whole, which is shorter than its diff:
```python
import functools

import jax
import jax.numpy as jnp
from jax import lax
from jax.experimental import pallas as pl
from jax.experimental.pallas import tpu as pltpu
from jax.sharding import PartitionSpec as P

ITERS = 4
LANES = 128
F32, BF16 = jnp.float32, jnp.bfloat16


def ring_partner(place, shift):
    return place ^ 1 if shift == 0 else 3 - place


def exchange(value, axis, partner):
    pairs = [(i, partner(i)) for i in range(lax.axis_size(axis))]
    return lax.ppermute(value, axis, pairs)


def col_block(value, shift):
    def at(flip_y, flip_x):
        def partner(i):
            y, x = divmod(i, 4)
            y = ring_partner(y, shift) if flip_y else y
            x = ring_partner(x, shift) if flip_x else x
            return y * 4 + x
        return partner
    across = exchange(value, "col", at(True, True))
    along_x = exchange(value, "col", at(False, True))
    along_y = exchange(value, "col", at(True, False))
    return (value, along_x, along_y, across)


def row_block(value):
    def turned(step):
        return lambda i: ((i // 2 + step) % 4) * 2 + i % 2
    far = exchange(value, "row", turned(2))
    up = exchange(value, "row", turned(1))
    down = exchange(value, "row", turned(3))
    return (value, far, up, down)


def total(terms):
    return (terms[0] + terms[1]) + (terms[2] + terms[3])


def sum_over_col(value):
    return col_block(total(col_block(value, 0)), 1)


def sum_over_row(value):
    return row_block(value + exchange(value, "row", lambda i: i ^ 1))


def chunks_of(refs, width):
    return [total([r[:, i:i + LANES] for r in refs]) for i in range(0, width, LANES)]


def whole_row(value, j):
    return jnp.broadcast_to(value[j:j + 1, :], value.shape)


def factored(gram, chunks):
    k = gram.shape[0]
    row = lax.broadcasted_iota(jnp.int32, (k, LANES), 0)
    lane = lax.broadcasted_iota(jnp.int32, (k, LANES), 1)
    columns = [jnp.broadcast_to(gram[:, j:j + 1], (k, LANES)) for j in range(k)]
    diagonal = jnp.zeros((k, LANES), F32)
    for j in range(k):
        pivot = whole_row(columns[j], j)
        inverse = lax.rsqrt(pivot)
        diagonal = jnp.where(lane == j, pivot * inverse, diagonal)
        column = columns[j] * inverse
        for i in range(j + 1, k):
            columns[i] = columns[i] - column * whole_row(column, i)
        below = jnp.where(row > j, column, 0.0)
        here = row == j
        solved = []
        for chunk in chunks:
            line = whole_row(chunk, j) * inverse
            solved.append(jnp.where(here, line, chunk - below * line))
        chunks = solved
    return diagonal, chunks


def store_terms(chunks, terms_ref):
    terms = terms_ref.shape[0] // 8
    for n, chunk in enumerate(chunks):
        parts = []
        for _ in range(terms):
            part = chunk.astype(BF16).astype(F32)
            parts.append(part)
            chunk = chunk - part
        terms_ref[:, n * LANES:(n + 1) * LANES] = jnp.concatenate(parts, 0).astype(BF16)


def rows_added(value):
    out = value[:8]
    for n in range(8, value.shape[0], 8):
        out = out + value[n:n + 8]
    return out


def contract(left, right, right_dim):
    return lax.dot_general(left, right, (((1,), (right_dim,)), ((), ())), preferred_element_type=F32)


def gram_of(terms_ref):
    everything = terms_ref[...]
    gram = None
    for n in range(0, terms_ref.shape[0], 8):
        part = rows_added(contract(everything, terms_ref[n:n + 8, :], 1))
        gram = part if gram is None else gram + part
    return gram


def product_into(out_ref, terms_ref, matrix_ref, right_dim):
    left = terms_ref[...]
    if right_dim == 0:
        out_ref[:, :matrix_ref.shape[1]] = rows_added(contract(left, matrix_ref[...], 0))
    else:
        step = 512
        for n in range(0, matrix_ref.shape[0], step):
            out_ref[:, n:n + step] = rows_added(contract(left, matrix_ref[n:n + step, :], 1))


def first_kernel(block_ref, matrix_ref, out_ref):
    out_ref[...] = contract(block_ref[...], matrix_ref[...], 0)


def step_kernel(normal, right_dim, last, *refs):
    refs = list(refs)
    terms = [refs.pop(0) for _ in range(4)]
    estimates_ref = refs.pop(0) if normal is not None else None
    matrix_ref = None if last else refs.pop(0)
    width = terms[0].shape[1]
    if normal is None:
        out_ref, split_ref = refs
        chunks = chunks_of(terms, width)
    else:
        width -= LANES
        gram = total([t[:, width:] for t in terms])
        if last:
            out_ref, block_ref, estimates_out, split_ref = refs
        else:
            out_ref, estimates_out, split_ref = refs
        diagonal, chunks = factored(gram, chunks_of(terms, width))
        row = lax.broadcasted_iota(jnp.int32, diagonal.shape, 0)
        estimates_out[...] = jnp.where(row == normal, diagonal, estimates_ref[...])
    store_terms(chunks, split_ref)
    gram = gram_of(split_ref)
    if last:
        for n, chunk in enumerate(chunks):
            block_ref[:, n * LANES:(n + 1) * LANES] = chunk
        at = 0
    else:
        product_into(out_ref, split_ref, matrix_ref, right_dim)
        at = out_ref.shape[1] - LANES
    out_ref[:, at:] = jnp.zeros((8, LANES), F32)
    out_ref[:, at:at + 8] = gram


def final_kernel(a_ref, b_ref, c_ref, d_ref, block_ref, estimates_ref, vectors_ref, estimates_out):
    gram = total([r[...] for r in (a_ref, b_ref, c_ref, d_ref)])
    width = block_ref.shape[1]
    chunks = [block_ref[:, n:n + LANES] for n in range(0, width, LANES)]
    diagonal, chunks = factored(gram, chunks)
    for n, chunk in enumerate(chunks):
        vectors_ref[:, n * LANES:(n + 1) * LANES] = chunk
    row = lax.broadcasted_iota(jnp.int32, diagonal.shape, 0)
    everything = jnp.where(row == ITERS - 1, diagonal, estimates_ref[...])
    estimates_out[...] = everything[:ITERS, :8]


def call(kernel, shapes, scratch, name, *args):
    vmem = pl.BlockSpec(memory_space=pltpu.VMEM)
    return pl.pallas_call(
        kernel,
        out_shape=[jax.ShapeDtypeStruct(s, F32) for s in shapes],
        in_specs=[vmem] * len(args),
        out_specs=[vmem] * len(shapes),
        scratch_shapes=[pltpu.VMEM(s, BF16) for s in scratch],
        compiler_params=pltpu.CompilerParams(vmem_limit_bytes=16 << 20),
        name=name,
    )(*args)


def shards(initial, matrix):
    rows, columns = matrix.shape
    k = initial.shape[0]
    matrix = pltpu.with_memory_space_constraint(matrix, pltpu.VMEM)
    copies = jnp.broadcast_to(initial, (lax.axis_size("col"), *initial.shape))
    pieces = lax.all_to_all(copies, "col", split_axis=0, concat_axis=0, tiled=True)
    block = jnp.moveaxis(pieces, 0, 1).reshape(k, rows)

    estimates = jnp.zeros((k, LANES), F32)
    (product,) = call(first_kernel, [(k, columns)], [], "product1", block, matrix)
    terms = sum_over_row(product)
    (product,) = call(
        functools.partial(step_kernel, None, 1, False),
        [(k, rows + LANES)], [(24, columns)], "product2", *terms, matrix)
    terms = sum_over_col(product)
    product, estimates = call(
        functools.partial(step_kernel, 0, 0, False),
        [(k, columns + LANES), (k, LANES)], [(16, rows)], "product3", *terms, estimates, matrix)
    terms = sum_over_row(product)
    product, estimates = call(
        functools.partial(step_kernel, 1, 1, False),
        [(k, rows + LANES), (k, LANES)], [(16, columns)], "product4", *terms, estimates, matrix)
    terms = sum_over_col(product)
    gram, block, estimates = call(
        functools.partial(step_kernel, 2, None, True),
        [(k, LANES), (k, rows), (k, LANES)], [(16, rows)], "last_gram", *terms, estimates)
    terms = sum_over_row(gram)
    own = rows // lax.axis_size("col")
    piece = lax.dynamic_slice_in_dim(block, lax.axis_index("col") * own, own, 1)
    piece = jnp.pad(piece, ((0, 0), (0, -own % LANES)))
    vectors, estimates = call(
        final_kernel, [(k, piece.shape[1]), (ITERS, k)], [], "final", *terms, piece, estimates)
    return (vectors[:, :own], estimates)


def solution(mesh):
    return jax.shard_map(
        shards,
        mesh=mesh,
        in_specs=(P(None, ("row", "col")), P("row", "col")),
        out_specs=(P(None, ("row", "col")), P()),
        check_vma=False,
    )
```

time: 170 us -> 93.2 us (0.55)
  blocking collectives: 119 us -> 14.6 us
  starting transfers between devices: 3.33 us -> 35.2 us
  waiting for transfers between devices: 3.44 us -> 28 us
  matrix products: 24.3 us -> 0 us
  other arithmetic: 11.6 us -> 0.07 us
  Pallas kernels: 0 us -> 9.78 us
    all_to_all x8 -> x1, blocking collectives: 119 us -> 14.6 us  [shards(): lax.all_to_all(copies, 'col', split_axis=0, concat_axis=0, tiled=True)]
    ppermute x0 -> x24, starting transfers between devices: none -> 35.2 us  [exchange(): return lax.ppermute(value, axis, pairs)]
    ppermute x0 -> x24, waiting for transfers between devices: none -> 28 us  [exchange(): return lax.ppermute(value, axis, pairs)]
    dot_general x8 -> x0, matrix products: 23.3 us -> none  [the longest x2 12.4 us: shards(): lax.dot_general(current, matrix, (((1,), (1,)), ((), ())), preferred_elem...]
    another operation x21 -> x0, other arithmetic: 11.3 us -> none  [the longest x12 5.57 us: normalise(): factor = jnp.linalg.cholesky(gram_matrix)]
    pallas_call x0 -> x6, Pallas kernels: none -> 9.78 us  [call(): pl.pallas_call(kernel, out_shape=[jax.ShapeDtypeStruct(s, F32) for s in s...]
    unnamed x0 -> x4, local copies, waits for them, and re-layouts: none -> 3.68 us
    all_to_all x1 -> x0, waiting for transfers between devices: 3.44 us -> none  [copy_for_each(): return lax.all_to_all(copies, axis, split_axis=0, concat_axis=0, tiled=True)]
  transfers between devices with their start and end apart: 1 -> 24, of which waited for: 1 -> 20; matrix products, arithmetic and copies ran while one was open for 1% -> 0% of each run, Pallas kernels for 0% -> 0%
where the time goes in v1:
time: 93.2 us; the launch traced here: 92.9 us
  starting transfers between devices  35.2 us (38%)
  waiting for transfers between devices  28 us (30%)
  blocking collectives  14.6 us (16%)
  Pallas kernels  9.78 us (10%)
  local copies, waits for them, and re-layouts  4.59 us (5%)
    ppermute x24, starting transfers between devices, exchange(): return lax.ppermute(value, axis, pairs)  35.2 us
    ppermute x24, waiting for transfers between devices, exchange(): return lax.ppermute(value, axis, pairs)  28 us
    all_to_all x1, blocking collectives, shards(): lax.all_to_all(copies, 'col', split_axis=0, concat_axis=0, tiled=True)  14.6 us
    pallas_call x6, Pallas kernels, call(): pl.pallas_call(kernel, out_shape=[jax.ShapeDtypeStruct(s, F32) for s in s...  9.78 us
    unnamed x4, local copies, waits for them, and re-layouts  3.68 us
  transfers between devices with their start and end apart: 24, of which 20 were waited for; matrix products, arithmetic and copies ran while one was open for 0% of the time, Pallas kernels for 0%

profile of v1, /device:TPU:0, one launch (start us, length us, event | category | flops | bytes accessed | tf_op | source)
XLA Modules:
  0.0 92.9 jit_solution(3596545900198909075)
XLA Ops:
  0.6 0.7 broadcast_in_dim.6
  1.3 14.6 %all_to_all.5 = bf16[16,8,192]{2,1,0:T(8,128)(2,1)S(1)} all-to-all(bf16[16,8,192]{2,1,0:T(8,128)(2,1)S(1)} %broadcast_in_dim.6), channel_id=1, replica_groups=mesh['row'=8,'col'=16] {'col'}, dimensions={0} | all-to-all | bytes 98304 | tf_op jit(solution)/shard_map/all_to_all | solution.py:197
  16.0 3.7 %copy-done = bf16[3072,1536]{1,0:T(8,128)(2,1)S(1)} copy-done((bf16[3072,1536]{1,0:T(8,128)(2,1)S(1)}, bf16[3072,1536]{1,0:T(8,128)(2,1)}, u32[]{:S(2)}) %copy-start) | copy-done | bytes 9437208
  19.7 1.3 %product1.1 = f32[8,1536]{1,0:T(8,128)S(1)} custom-call(bf16[8,3072]{1,0:T(8,128)(2,1)S(1)} %reshape.7.block_ref, bf16[3072,1536]{1,0:T(8,128)(2,1)S(1)} %copy-done), custom_call_target="tpu_custom_call" | custom-call | tf_op jit(solution)/shard_map/product1/pallas_call | solution.py:181
  21.0 1.2 %collective-permute-done = f32[8,1536]{1,0:T(8,128)S(1)} collective-permute-done((f32[8,1536]{1,0:T(8,128)S(1)}, f32[8,1536]{1,0:T(8,128)S(1)}, u32[]{:S(2)}, u32[]{:S(2)}) %collective-permute-start) | collective-permute-done | bytes 49184 | tf_op jit(solution)/shard_map/ppermute | solution.py:21
  22.3 3.9 %collective-permute-start.1 = (f32[8,1536]{1,0:T(8,128)S(1)}, f32[8,1536]{1,0:T(8,128)S(1)}, u32[]{:S(2)}, u32[]{:S(2)}) collective-permute-start(f32[8,1536]{1,0:T(8,128)S(1)} %add.32.refs_0_), channel_id=1, source_target_pairs={{0,64},{16,80},{32,96},{48,112},{64,0},{80,16},{96,32},{112,48},{1... | collective-permute-start | bytes 147464 | tf_op jit(solution)/shard_map/ppermute | solution.py:21
  26.2 1.0 %collective-permute-start.2 = (f32[8,1536]{1,0:T(8,128)S(1)}, f32[8,1536]{1,0:T(8,128)S(1)}, u32[]{:S(2)}, u32[]{:S(2)}) collective-permute-start(f32[8,1536]{1,0:T(8,128)S(1)} %add.32.refs_0_), channel_id=1, source_target_pairs={{0,32},{16,48},{32,64},{48,80},{64,96},{80,112},{96,0},{112,16},{1... | collective-permute-start | bytes 147464 | tf_op jit(solution)/shard_map/ppermute | solution.py:21
  27.3 2.2 %collective-permute-start.3 = (f32[8,1536]{1,0:T(8,128)S(1)}, f32[8,1536]{1,0:T(8,128)S(1)}, u32[]{:S(2)}, u32[]{:S(2)}) collective-permute-start(f32[8,1536]{1,0:T(8,128)S(1)} %add.32.refs_0_), channel_id=1, source_target_pairs={{0,96},{16,112},{32,0},{48,16},{64,32},{80,48},{96,64},{112,80},{1... | collective-permute-start | bytes 147464 | tf_op jit(solution)/shard_map/ppermute | solution.py:21
  29.5 2.1 %collective-permute-done.2.refs_2_ = f32[8,1536]{1,0:T(8,128)S(1)} collective-permute-done((f32[8,1536]{1,0:T(8,128)S(1)}, f32[8,1536]{1,0:T(8,128)S(1)}, u32[]{:S(2)}, u32[]{:S(2)}) %collective-permute-start.2) | collective-permute-done | bytes 49184 | tf_op jit(solution)/shard_map/ppermute | solution.py:21
  31.5 2.9 %product2.1 = f32[8,3200]{1,0:T(8,128)S(1)} custom-call(f32[8,1536]{1,0:T(8,128)S(1)} %add.32.refs_0_, f32[8,1536]{1,0:T(8,128)S(1)} %collective-permute-done.1.refs_1_, f32[8,1536]{1,0:T(8,128)S(1)} %collective-permute-done.2.refs_2_, f32[8,1536]{1,0:T(8,128)S(1)} %collective-permute-done.3.refs_3_, bf16[3072,1536]{1,0:T(8,128)(2,1)S(1)} %copy-done.1), custom_call_target="tpu_custom_call" | custom-call | tf_op jit(solution)/shard_map/product2/pallas_call | solution.py:181
  34.5 0.6 collective-permute-start.4
  35.1 0.5 collective-permute-start.5
  35.6 2.4 %collective-permute-start.6 = (f32[8,3200]{1,0:T(8,128)S(1)}, f32[8,3200]{1,0:T(8,128)S(1)}, u32[]{:S(2)}, u32[]{:S(2)}) collective-permute-start(f32[8,3200]{1,0:T(8,128)S(1)} %product2.1), channel_id=1, source_target_pairs={{0,5},{1,4},{2,7},{3,6},{4,1},{5,0},{6,3},{7,2},{8,13},{9,12},{10,... | collective-permute-start | bytes 307208 | tf_op jit(solution)/shard_map/ppermute | solution.py:21
  38.1 1.4 %collective-permute-done.4 = f32[8,3200]{1,0:T(8,128)S(1)} collective-permute-done((f32[8,3200]{1,0:T(8,128)S(1)}, f32[8,3200]{1,0:T(8,128)S(1)}, u32[]{:S(2)}, u32[]{:S(2)}) %collective-permute-start.4) | collective-permute-done | bytes 102432 | tf_op jit(solution)/shard_map/ppermute | solution.py:21
  39.5 0.3 collective-permute-done.5
  39.8 1.4 %collective-permute-done.6 = f32[8,3200]{1,0:T(8,128)S(1)} collective-permute-done((f32[8,3200]{1,0:T(8,128)S(1)}, f32[8,3200]{1,0:T(8,128)S(1)}, u32[]{:S(2)}, u32[]{:S(2)}) %collective-permute-start.6) | collective-permute-done | bytes 102432 | tf_op jit(solution)/shard_map/ppermute | solution.py:21
  41.2 1.4 %collective-permute-start.7 = (f32[8,3200]{1,0:T(8,128)S(1)}, f32[8,3200]{1,0:T(8,128)S(1)}, u32[]{:S(2)}, u32[]{:S(2)}) collective-permute-start(f32[8,3200]{1,0:T(8,128)S(1)} %add_add_fusion.1.refs_0_), channel_id=1, source_target_pairs={{0,3},{1,2},{2,1},{3,0},{4,7},{5,6},{6,5},{7,4},{8,11},{9,10},{10,... | collective-permute-start | bytes 307208 | tf_op jit(solution)/shard_map/ppermute | solution.py:21
  42.7 1.2 %collective-permute-start.8 = (f32[8,3200]{1,0:T(8,128)S(1)}, f32[8,3200]{1,0:T(8,128)S(1)}, u32[]{:S(2)}, u32[]{:S(2)}) collective-permute-start(f32[8,3200]{1,0:T(8,128)S(1)} %add_add_fusion.1.refs_0_), channel_id=1, source_target_pairs={{0,12},{1,13},{2,14},{3,15},{4,8},{5,9},{6,10},{7,11},{8,4},{9,5},... | collective-permute-start | bytes 307208 | tf_op jit(solution)/shard_map/ppermute | solution.py:21
  43.9 3.4 %collective-permute-start.9 = (f32[8,3200]{1,0:T(8,128)S(1)}, f32[8,3200]{1,0:T(8,128)S(1)}, u32[]{:S(2)}, u32[]{:S(2)}) collective-permute-start(f32[8,3200]{1,0:T(8,128)S(1)} %add_add_fusion.1.refs_0_), channel_id=1, source_target_pairs={{0,15},{1,14},{2,13},{3,12},{4,11},{5,10},{6,9},{7,8},{8,7},{9,6},... | collective-permute-start | bytes 307208 | tf_op jit(solution)/shard_map/ppermute | solution.py:21
  47.2 0.9 collective-permute-done.7.refs_1_
  48.2 1.0 %collective-permute-done.8.refs_2_ = f32[8,3200]{1,0:T(8,128)S(1)} collective-permute-done((f32[8,3200]{1,0:T(8,128)S(1)}, f32[8,3200]{1,0:T(8,128)S(1)}, u32[]{:S(2)}, u32[]{:S(2)}) %collective-permute-start.8) | collective-permute-done | bytes 102432 | tf_op jit(solution)/shard_map/ppermute | solution.py:21
  49.2 2.7 %collective-permute-done.9.refs_3_ = f32[8,3200]{1,0:T(8,128)S(1)} collective-permute-done((f32[8,3200]{1,0:T(8,128)S(1)}, f32[8,3200]{1,0:T(8,128)S(1)}, u32[]{:S(2)}, u32[]{:S(2)}) %collective-permute-start.9) | collective-permute-done | bytes 102432 | tf_op jit(solution)/shard_map/ppermute | solution.py:21
  51.9 1.6 %product3.1 = (f32[8,1664]{1,0:T(8,128)S(1)}, f32[8,128]{1,0:T(8,128)S(1)}) custom-call(f32[8,3200]{1,0:T(8,128)S(1)} %add_add_fusion.1.refs_0_, f32[8,3200]{1,0:T(8,128)S(1)} %collective-permute-done.7.refs_1_, f32[8,3200]{1,0:T(8,128)S(1)} %collective-permute-done.8.refs_2_, f32[8,3200]{1,0:T(8,128)S(1)} %collective-permute-done.9.refs_3_, ...), custom_call_target="tpu_custom_call" | custom-call | tf_op jit(solution)/shard_map/product3/pallas_call | solution.py:181
  53.5 1.2 %collective-permute-done.10 = f32[8,1664]{1,0:T(8,128)S(1)} collective-permute-done((f32[8,1664]{1,0:T(8,128)S(1)}, f32[8,1664]{1,0:T(8,128)S(1)}, u32[]{:S(2)}, u32[]{:S(2)}) %collective-permute-start.10) | collective-permute-done | bytes 53280 | tf_op jit(solution)/shard_map/ppermute | solution.py:21
  54.7 1.5 %collective-permute-start.11 = (f32[8,1664]{1,0:T(8,128)S(1)}, f32[8,1664]{1,0:T(8,128)S(1)}, u32[]{:S(2)}, u32[]{:S(2)}) collective-permute-start(f32[8,1664]{1,0:T(8,128)S(1)} %add.36.refs_0_), channel_id=1, source_target_pairs={{0,64},{16,80},{32,96},{48,112},{64,0},{80,16},{96,32},{112,48},{1... | collective-permute-start | bytes 159752 | tf_op jit(solution)/shard_map/ppermute | solution.py:21
  56.3 2.6 %collective-permute-start.12 = (f32[8,1664]{1,0:T(8,128)S(1)}, f32[8,1664]{1,0:T(8,128)S(1)}, u32[]{:S(2)}, u32[]{:S(2)}) collective-permute-start(f32[8,1664]{1,0:T(8,128)S(1)} %add.36.refs_0_), channel_id=1, source_target_pairs={{0,32},{16,48},{32,64},{48,80},{64,96},{80,112},{96,0},{112,16},{1... | collective-permute-start | bytes 159752 | tf_op jit(solution)/shard_map/ppermute | solution.py:21
  58.9 0.6 collective-permute-start.13
  59.5 1.2 %collective-permute-done.11.refs_1_ = f32[8,1664]{1,0:T(8,128)S(1)} collective-permute-done((f32[8,1664]{1,0:T(8,128)S(1)}, f32[8,1664]{1,0:T(8,128)S(1)}, u32[]{:S(2)}, u32[]{:S(2)}) %collective-permute-start.11) | collective-permute-done | bytes 53280 | tf_op jit(solution)/shard_map/ppermute | solution.py:21
  60.7 0.9 collective-permute-done.12.refs_2_
  61.6 1.4 %collective-permute-done.13.refs_3_ = f32[8,1664]{1,0:T(8,128)S(1)} collective-permute-done((f32[8,1664]{1,0:T(8,128)S(1)}, f32[8,1664]{1,0:T(8,128)S(1)}, u32[]{:S(2)}, u32[]{:S(2)}) %collective-permute-start.13) | collective-permute-done | bytes 53280 | tf_op jit(solution)/shard_map/ppermute | solution.py:21
  63.1 2.7 %product4.1 = (f32[8,3200]{1,0:T(8,128)S(1)}, f32[8,128]{1,0:T(8,128)S(1)}) custom-call(f32[8,1664]{1,0:T(8,128)S(1)} %add.36.refs_0_, f32[8,1664]{1,0:T(8,128)S(1)} %collective-permute-done.11.refs_1_, f32[8,1664]{1,0:T(8,128)S(1)} %collective-permute-done.12.refs_2_, f32[8,1664]{1,0:T(8,128)S(1)} %collective-permute-done.13.refs_3_, ...), custom_call_target="tpu_custom_call" | custom-call | tf_op jit(solution)/shard_map/product4/pallas_call | solution.py:181
  65.9 3.4 %collective-permute-start.16 = (f32[8,3200]{1,0:T(8,128)S(1)}, f32[8,3200]{1,0:T(8,128)S(1)}, u32[]{:S(2)}, u32[]{:S(2)}) collective-permute-start(f32[8,3200]{1,0:T(8,128)S(1)} %get-tuple-element.13), channel_id=1, source_target_pairs={{0,5},{1,4},{2,7},{3,6},{4,1},{5,0},{6,3},{7,2},{8,13},{9,12},{10,... | collective-permute-start | bytes 307208 | tf_op jit(solution)/shard_map/ppermute | solution.py:21
  69.3 1.3 %collective-permute-done.14 = f32[8,3200]{1,0:T(8,128)S(1)} collective-permute-done((f32[8,3200]{1,0:T(8,128)S(1)}, f32[8,3200]{1,0:T(8,128)S(1)}, u32[]{:S(2)}, u32[]{:S(2)}) %collective-permute-start.14) | collective-permute-done | bytes 102432 | tf_op jit(solution)/shard_map/ppermute | solution.py:21
  70.6 1.5 %collective-permute-done.15 = f32[8,3200]{1,0:T(8,128)S(1)} collective-permute-done((f32[8,3200]{1,0:T(8,128)S(1)}, f32[8,3200]{1,0:T(8,128)S(1)}, u32[]{:S(2)}, u32[]{:S(2)}) %collective-permute-start.15) | collective-permute-done | bytes 102432 | tf_op jit(solution)/shard_map/ppermute | solution.py:21
  72.1 2.0 %collective-permute-start.17 = (f32[8,3200]{1,0:T(8,128)S(1)}, f32[8,3200]{1,0:T(8,128)S(1)}, u32[]{:S(2)}, u32[]{:S(2)}) collective-permute-start(f32[8,3200]{1,0:T(8,128)S(1)} %add_add_fusion.refs_0_), channel_id=1, source_target_pairs={{0,3},{1,2},{2,1},{3,0},{4,7},{5,6},{6,5},{7,4},{8,11},{9,10},{10,... | collective-permute-start | bytes 307208 | tf_op jit(solution)/shard_map/ppermute | solution.py:21
  74.1 2.0 %collective-permute-start.18 = (f32[8,3200]{1,0:T(8,128)S(1)}, f32[8,3200]{1,0:T(8,128)S(1)}, u32[]{:S(2)}, u32[]{:S(2)}) collective-permute-start(f32[8,3200]{1,0:T(8,128)S(1)} %add_add_fusion.refs_0_), channel_id=1, source_target_pairs={{0,12},{1,13},{2,14},{3,15},{4,8},{5,9},{6,10},{7,11},{8,4},{9,5},... | collective-permute-start | bytes 307208 | tf_op jit(solution)/shard_map/ppermute | solution.py:21
  76.1 2.0 %collective-permute-start.19 = (f32[8,3200]{1,0:T(8,128)S(1)}, f32[8,3200]{1,0:T(8,128)S(1)}, u32[]{:S(2)}, u32[]{:S(2)}) collective-permute-start(f32[8,3200]{1,0:T(8,128)S(1)} %add_add_fusion.refs_0_), channel_id=1, source_target_pairs={{0,15},{1,14},{2,13},{3,12},{4,11},{5,10},{6,9},{7,8},{8,7},{9,6},... | collective-permute-start | bytes 307208 | tf_op jit(solution)/shard_map/ppermute | solution.py:21
  78.1 2.9 %collective-permute-done.18.refs_2_ = f32[8,3200]{1,0:T(8,128)S(1)} collective-permute-done((f32[8,3200]{1,0:T(8,128)S(1)}, f32[8,3200]{1,0:T(8,128)S(1)}, u32[]{:S(2)}, u32[]{:S(2)}) %collective-permute-start.18) | collective-permute-done | bytes 102432 | tf_op jit(solution)/shard_map/ppermute | solution.py:21
  81.1 3.0 %collective-permute-done.19.refs_3_ = f32[8,3200]{1,0:T(8,128)S(1)} collective-permute-done((f32[8,3200]{1,0:T(8,128)S(1)}, f32[8,3200]{1,0:T(8,128)S(1)}, u32[]{:S(2)}, u32[]{:S(2)}) %collective-permute-start.19) | collective-permute-done | bytes 102432 | tf_op jit(solution)/shard_map/ppermute | solution.py:21
  84.1 0.4 last_gram.1
  84.5 1.2 %collective-permute-done.20 = f32[8,128]{1,0:T(8,128)S(1)} collective-permute-done((f32[8,128]{1,0:T(8,128)S(1)}, f32[8,128]{1,0:T(8,128)S(1)}, u32[]{:S(2)}, u32[]{:S(2)}) %collective-permute-start.20) | collective-permute-done | bytes 4128 | tf_op jit(solution)/shard_map/ppermute | solution.py:21
  85.7 0.9 %collective-permute-start.21 = (f32[8,128]{1,0:T(8,128)S(1)}, f32[8,128]{1,0:T(8,128)S(1)}, u32[]{:S(2)}, u32[]{:S(2)}) collective-permute-start(f32[8,128]{1,0:T(8,128)S(1)} %add.40.a_ref), channel_id=1, source_target_pairs={{0,64},{16,80},{32,96},{48,112},{64,0},{80,16},{96,32},{112,48},{1... | collective-permute-start | bytes 12296 | tf_op jit(solution)/shard_map/ppermute | solution.py:21
  86.6 2.0 %collective-permute-start.22 = (f32[8,128]{1,0:T(8,128)S(1)}, f32[8,128]{1,0:T(8,128)S(1)}, u32[]{:S(2)}, u32[]{:S(2)}) collective-permute-start(f32[8,128]{1,0:T(8,128)S(1)} %add.40.a_ref), channel_id=1, source_target_pairs={{0,32},{16,48},{32,64},{48,80},{64,96},{80,112},{96,0},{112,16},{1... | collective-permute-start | bytes 12296 | tf_op jit(solution)/shard_map/ppermute | solution.py:21
  88.6 1.2 %collective-permute-start.23 = (f32[8,128]{1,0:T(8,128)S(1)}, f32[8,128]{1,0:T(8,128)S(1)}, u32[]{:S(2)}, u32[]{:S(2)}) collective-permute-start(f32[8,128]{1,0:T(8,128)S(1)} %add.40.a_ref), channel_id=1, source_target_pairs={{0,96},{16,112},{32,0},{48,16},{64,32},{80,48},{96,64},{112,80},{1... | collective-permute-start | bytes 12296 | tf_op jit(solution)/shard_map/ppermute | solution.py:21
  89.9 0.9 collective-permute-done.21.b_ref
  90.8 0.6 collective-permute-done.22.c_ref
  91.4 0.8 collective-permute-done.23.d_ref
  92.2 0.8 final.1
  (22 shorter events, 0.4 us)
Async XLA Ops:
  16.0 3.7 %copy-start = (bf16[3072,1536]{1,0:T(8,128)(2,1)S(1)}, bf16[3072,1536]{1,0:T(8,128)(2,1)}, u32[]{:S(2)}) copy-start(bf16[3072,1536]{1,0:T(8,128)(2,1)} %refs_5_.3) | copy-start | bytes 28311556
  19.7 11.8 %copy-start.1 = (bf16[3072,1536]{1,0:T(8,128)(2,1)S(1)}, bf16[3072,1536]{1,0:T(8,128)(2,1)}, u32[]{:S(2)}) copy-start(bf16[3072,1536]{1,0:T(8,128)(2,1)} %refs_5_.3) | copy-start | bytes 28311556
  21.0 1.2 %collective-permute-start = (f32[8,1536]{1,0:T(8,128)S(1)}, f32[8,1536]{1,0:T(8,128)S(1)}, u32[]{:S(2)}, u32[]{:S(2)}) collective-permute-start(f32[8,1536]{1,0:T(8,128)S(1)} %product1.1), channel_id=1, source_target_pairs={{0,16},{16,0},{32,48},{48,32},{64,80},{80,64},{96,112},{112,96},{1... | collective-permute-start | bytes 147464 | tf_op jit(solution)/shard_map/ppermute | solution.py:21
  22.3 7.2 %collective-permute-start.1 = (f32[8,1536]{1,0:T(8,128)S(1)}, f32[8,1536]{1,0:T(8,128)S(1)}, u32[]{:S(2)}, u32[]{:S(2)}) collective-permute-start(f32[8,1536]{1,0:T(8,128)S(1)} %add.32.refs_0_), channel_id=1, source_target_pairs={{0,64},{16,80},{32,96},{48,112},{64,0},{80,16},{96,32},{112,48},{1... | collective-permute-start | bytes 147464 | tf_op jit(solution)/shard_map/ppermute | solution.py:21
  26.2 5.3 %collective-permute-start.2 = (f32[8,1536]{1,0:T(8,128)S(1)}, f32[8,1536]{1,0:T(8,128)S(1)}, u32[]{:S(2)}, u32[]{:S(2)}) collective-permute-start(f32[8,1536]{1,0:T(8,128)S(1)} %add.32.refs_0_), channel_id=1, source_target_pairs={{0,32},{16,48},{32,64},{48,80},{64,96},{80,112},{96,0},{112,16},{1... | collective-permute-start | bytes 147464 | tf_op jit(solution)/shard_map/ppermute | solution.py:21
  27.3 4.3 %collective-permute-start.3 = (f32[8,1536]{1,0:T(8,128)S(1)}, f32[8,1536]{1,0:T(8,128)S(1)}, u32[]{:S(2)}, u32[]{:S(2)}) collective-permute-start(f32[8,1536]{1,0:T(8,128)S(1)} %add.32.refs_0_), channel_id=1, source_target_pairs={{0,96},{16,112},{32,0},{48,16},{64,32},{80,48},{96,64},{112,80},{1... | collective-permute-start | bytes 147464 | tf_op jit(solution)/shard_map/ppermute | solution.py:21
  34.5 5.0 %collective-permute-start.4 = (f32[8,3200]{1,0:T(8,128)S(1)}, f32[8,3200]{1,0:T(8,128)S(1)}, u32[]{:S(2)}, u32[]{:S(2)}) collective-permute-start(f32[8,3200]{1,0:T(8,128)S(1)} %product2.1), channel_id=1, source_target_pairs={{0,1},{1,0},{2,3},{3,2},{4,5},{5,4},{6,7},{7,6},{8,9},{9,8},{10,11... | collective-permute-start | bytes 307208 | tf_op jit(solution)/shard_map/ppermute | solution.py:21
  35.1 4.7 %collective-permute-start.5 = (f32[8,3200]{1,0:T(8,128)S(1)}, f32[8,3200]{1,0:T(8,128)S(1)}, u32[]{:S(2)}, u32[]{:S(2)}) collective-permute-start(f32[8,3200]{1,0:T(8,128)S(1)} %product2.1), channel_id=1, source_target_pairs={{0,4},{1,5},{2,6},{3,7},{4,0},{5,1},{6,2},{7,3},{8,12},{9,13},{10,... | collective-permute-start | bytes 307208 | tf_op jit(solution)/shard_map/ppermute | solution.py:21
  35.6 5.6 %collective-permute-start.6 = (f32[8,3200]{1,0:T(8,128)S(1)}, f32[8,3200]{1,0:T(8,128)S(1)}, u32[]{:S(2)}, u32[]{:S(2)}) collective-permute-start(f32[8,3200]{1,0:T(8,128)S(1)} %product2.1), channel_id=1, source_target_pairs={{0,5},{1,4},{2,7},{3,6},{4,1},{5,0},{6,3},{7,2},{8,13},{9,12},{10,... | collective-permute-start | bytes 307208 | tf_op jit(solution)/shard_map/ppermute | solution.py:21
  41.2 6.9 %collective-permute-start.7 = (f32[8,3200]{1,0:T(8,128)S(1)}, f32[8,3200]{1,0:T(8,128)S(1)}, u32[]{:S(2)}, u32[]{:S(2)}) collective-permute-start(f32[8,3200]{1,0:T(8,128)S(1)} %add_add_fusion.1.refs_0_), channel_id=1, source_target_pairs={{0,3},{1,2},{2,1},{3,0},{4,7},{5,6},{6,5},{7,4},{8,11},{9,10},{10,... | collective-permute-start | bytes 307208 | tf_op jit(solution)/shard_map/ppermute | solution.py:21
  42.7 6.5 %collective-permute-start.8 = (f32[8,3200]{1,0:T(8,128)S(1)}, f32[8,3200]{1,0:T(8,128)S(1)}, u32[]{:S(2)}, u32[]{:S(2)}) collective-permute-start(f32[8,3200]{1,0:T(8,128)S(1)} %add_add_fusion.1.refs_0_), channel_id=1, source_target_pairs={{0,12},{1,13},{2,14},{3,15},{4,8},{5,9},{6,10},{7,11},{8,4},{9,5},... | collective-permute-start | bytes 307208 | tf_op jit(solution)/shard_map/ppermute | solution.py:21
  43.9 8.0 %collective-permute-start.9 = (f32[8,3200]{1,0:T(8,128)S(1)}, f32[8,3200]{1,0:T(8,128)S(1)}, u32[]{:S(2)}, u32[]{:S(2)}) collective-permute-start(f32[8,3200]{1,0:T(8,128)S(1)} %add_add_fusion.1.refs_0_), channel_id=1, source_target_pairs={{0,15},{1,14},{2,13},{3,12},{4,11},{5,10},{6,9},{7,8},{8,7},{9,6},... | collective-permute-start | bytes 307208 | tf_op jit(solution)/shard_map/ppermute | solution.py:21
  53.5 1.2 %collective-permute-start.10 = (f32[8,1664]{1,0:T(8,128)S(1)}, f32[8,1664]{1,0:T(8,128)S(1)}, u32[]{:S(2)}, u32[]{:S(2)}) collective-permute-start(f32[8,1664]{1,0:T(8,128)S(1)} %get-tuple-element.11), channel_id=1, source_target_pairs={{0,16},{16,0},{32,48},{48,32},{64,80},{80,64},{96,112},{112,96},{1... | collective-permute-start | bytes 159752 | tf_op jit(solution)/shard_map/ppermute | solution.py:21
  54.7 6.0 %collective-permute-start.11 = (f32[8,1664]{1,0:T(8,128)S(1)}, f32[8,1664]{1,0:T(8,128)S(1)}, u32[]{:S(2)}, u32[]{:S(2)}) collective-permute-start(f32[8,1664]{1,0:T(8,128)S(1)} %add.36.refs_0_), channel_id=1, source_target_pairs={{0,64},{16,80},{32,96},{48,112},{64,0},{80,16},{96,32},{112,48},{1... | collective-permute-start | bytes 159752 | tf_op jit(solution)/shard_map/ppermute | solution.py:21
  56.3 5.3 %collective-permute-start.12 = (f32[8,1664]{1,0:T(8,128)S(1)}, f32[8,1664]{1,0:T(8,128)S(1)}, u32[]{:S(2)}, u32[]{:S(2)}) collective-permute-start(f32[8,1664]{1,0:T(8,128)S(1)} %add.36.refs_0_), channel_id=1, source_target_pairs={{0,32},{16,48},{32,64},{48,80},{64,96},{80,112},{96,0},{112,16},{1... | collective-permute-start | bytes 159752 | tf_op jit(solution)/shard_map/ppermute | solution.py:21
  58.9 4.1 %collective-permute-start.13 = (f32[8,1664]{1,0:T(8,128)S(1)}, f32[8,1664]{1,0:T(8,128)S(1)}, u32[]{:S(2)}, u32[]{:S(2)}) collective-permute-start(f32[8,1664]{1,0:T(8,128)S(1)} %add.36.refs_0_), channel_id=1, source_target_pairs={{0,96},{16,112},{32,0},{48,16},{64,32},{80,48},{96,64},{112,80},{1... | collective-permute-start | bytes 159752 | tf_op jit(solution)/shard_map/ppermute | solution.py:21
  65.8 4.8 %collective-permute-start.14 = (f32[8,3200]{1,0:T(8,128)S(1)}, f32[8,3200]{1,0:T(8,128)S(1)}, u32[]{:S(2)}, u32[]{:S(2)}) collective-permute-start(f32[8,3200]{1,0:T(8,128)S(1)} %get-tuple-element.13), channel_id=1, source_target_pairs={{0,1},{1,0},{2,3},{3,2},{4,5},{5,4},{6,7},{7,6},{8,9},{9,8},{10,11... | collective-permute-start | bytes 307208 | tf_op jit(solution)/shard_map/ppermute | solution.py:21
  65.8 6.3 %collective-permute-start.15 = (f32[8,3200]{1,0:T(8,128)S(1)}, f32[8,3200]{1,0:T(8,128)S(1)}, u32[]{:S(2)}, u32[]{:S(2)}) collective-permute-start(f32[8,3200]{1,0:T(8,128)S(1)} %get-tuple-element.13), channel_id=1, source_target_pairs={{0,4},{1,5},{2,6},{3,7},{4,0},{5,1},{6,2},{7,3},{8,12},{9,13},{10,... | collective-permute-start | bytes 307208 | tf_op jit(solution)/shard_map/ppermute | solution.py:21
  65.9 6.2 %collective-permute-start.16 = (f32[8,3200]{1,0:T(8,128)S(1)}, f32[8,3200]{1,0:T(8,128)S(1)}, u32[]{:S(2)}, u32[]{:S(2)}) collective-permute-start(f32[8,3200]{1,0:T(8,128)S(1)} %get-tuple-element.13), channel_id=1, source_target_pairs={{0,5},{1,4},{2,7},{3,6},{4,1},{5,0},{6,3},{7,2},{8,13},{9,12},{10,... | collective-permute-start | bytes 307208 | tf_op jit(solution)/shard_map/ppermute | solution.py:21
  72.1 6.0 %collective-permute-start.17 = (f32[8,3200]{1,0:T(8,128)S(1)}, f32[8,3200]{1,0:T(8,128)S(1)}, u32[]{:S(2)}, u32[]{:S(2)}) collective-permute-start(f32[8,3200]{1,0:T(8,128)S(1)} %add_add_fusion.refs_0_), channel_id=1, source_target_pairs={{0,3},{1,2},{2,1},{3,0},{4,7},{5,6},{6,5},{7,4},{8,11},{9,10},{10,... | collective-permute-start | bytes 307208 | tf_op jit(solution)/shard_map/ppermute | solution.py:21
  74.1 7.0 %collective-permute-start.18 = (f32[8,3200]{1,0:T(8,128)S(1)}, f32[8,3200]{1,0:T(8,128)S(1)}, u32[]{:S(2)}, u32[]{:S(2)}) collective-permute-start(f32[8,3200]{1,0:T(8,128)S(1)} %add_add_fusion.refs_0_), channel_id=1, source_target_pairs={{0,12},{1,13},{2,14},{3,15},{4,8},{5,9},{6,10},{7,11},{8,4},{9,5},... | collective-permute-start | bytes 307208 | tf_op jit(solution)/shard_map/ppermute | solution.py:21
  76.1 8.0 %collective-permute-start.19 = (f32[8,3200]{1,0:T(8,128)S(1)}, f32[8,3200]{1,0:T(8,128)S(1)}, u32[]{:S(2)}, u32[]{:S(2)}) collective-permute-start(f32[8,3200]{1,0:T(8,128)S(1)} %add_add_fusion.refs_0_), channel_id=1, source_target_pairs={{0,15},{1,14},{2,13},{3,12},{4,11},{5,10},{6,9},{7,8},{8,7},{9,6},... | collective-permute-start | bytes 307208 | tf_op jit(solution)/shard_map/ppermute | solution.py:21
  84.5 1.2 %collective-permute-start.20 = (f32[8,128]{1,0:T(8,128)S(1)}, f32[8,128]{1,0:T(8,128)S(1)}, u32[]{:S(2)}, u32[]{:S(2)}) collective-permute-start(f32[8,128]{1,0:T(8,128)S(1)} %get-tuple-element.15), channel_id=1, source_target_pairs={{0,16},{16,0},{32,48},{48,32},{64,80},{80,64},{96,112},{112,96},{1... | collective-permute-start | bytes 12296 | tf_op jit(solution)/shard_map/ppermute | solution.py:21
  85.7 5.1 %collective-permute-start.21 = (f32[8,128]{1,0:T(8,128)S(1)}, f32[8,128]{1,0:T(8,128)S(1)}, u32[]{:S(2)}, u32[]{:S(2)}) collective-permute-start(f32[8,128]{1,0:T(8,128)S(1)} %add.40.a_ref), channel_id=1, source_target_pairs={{0,64},{16,80},{32,96},{48,112},{64,0},{80,16},{96,32},{112,48},{1... | collective-permute-start | bytes 12296 | tf_op jit(solution)/shard_map/ppermute | solution.py:21
  86.6 4.8 %collective-permute-start.22 = (f32[8,128]{1,0:T(8,128)S(1)}, f32[8,128]{1,0:T(8,128)S(1)}, u32[]{:S(2)}, u32[]{:S(2)}) collective-permute-start(f32[8,128]{1,0:T(8,128)S(1)} %add.40.a_ref), channel_id=1, source_target_pairs={{0,32},{16,48},{32,64},{48,80},{64,96},{80,112},{96,0},{112,16},{1... | collective-permute-start | bytes 12296 | tf_op jit(solution)/shard_map/ppermute | solution.py:21
  88.6 3.6 %collective-permute-start.23 = (f32[8,128]{1,0:T(8,128)S(1)}, f32[8,128]{1,0:T(8,128)S(1)}, u32[]{:S(2)}, u32[]{:S(2)}) collective-permute-start(f32[8,128]{1,0:T(8,128)S(1)} %add.40.a_ref), channel_id=1, source_target_pairs={{0,96},{16,112},{32,0},{48,16},{64,32},{80,48},{96,64},{112,80},{1... | collective-permute-start | bytes 12296 | tf_op jit(solution)/shard_map/ppermute | solution.py:21

commit v2 on v1

--- a/solution.py
+++ b/solution.py
@@ -22,17 +22,14 @@
 
 
 def col_block(value, shift):
-    def at(flip_y, flip_x):
-        def partner(i):
-            y, x = divmod(i, 4)
-            y = ring_partner(y, shift) if flip_y else y
-            x = ring_partner(x, shift) if flip_x else x
-            return y * 4 + x
-        return partner
-    across = exchange(value, "col", at(True, True))
-    along_x = exchange(value, "col", at(False, True))
-    along_y = exchange(value, "col", at(True, False))
-    return (value, along_x, along_y, across)
+    def turned(step):
+        if shift == 0:
+            return lambda i: i // 4 * 4 + (i + step) % 4
+        return lambda i: (i + 4 * step) % 16
+    far = exchange(value, "col", turned(2))
+    up = exchange(value, "col", turned(1))
+    down = exchange(value, "col", turned(3))
+    return (value, far, up, down)
 
 
 def row_block(value):
@@ -128,8 +125,43 @@
             out_ref[:, n:n + step] = rows_added(contract(left, matrix_ref[n:n + step, :], 1))
 
 
-def first_kernel(block_ref, matrix_ref, out_ref):
-    out_ref[...] = contract(block_ref[...], matrix_ref[...], 0)
+PARTS = 12
+
+
+def first_kernel(pieces_ref, matrix_ref, out_ref, held_ref, block_ref, arrived):
+    size = matrix_ref.shape[0] // PARTS
+    own = pieces_ref.shape[2]
+    copies = []
+    for n in range(PARTS):
+        part = pl.ds(n * size, size)
+        copies.append(pltpu.make_async_copy(matrix_ref.at[part], held_ref.at[part], arrived.at[n]))
+        copies[-1].start()
+    for n in range(pieces_ref.shape[0]):
+        block_ref[:, n * own:(n + 1) * own] = pieces_ref[n].astype(F32)
+    product = None
+    for n, copy in enumerate(copies):
+        copy.wait()
+        part = slice(n * size, (n + 1) * size)
+        term = contract(block_ref[:, part].astype(BF16), held_ref[part, :], 0)
+        product = term if product is None else product + term
+    out_ref[...] = product
+
+
+def first_product(pieces, matrix):
+    pieces_count, k, own = pieces.shape
+    vmem = pl.BlockSpec(memory_space=pltpu.VMEM)
+    return pl.pallas_call(
+        first_kernel,
+        out_shape=[
+            jax.ShapeDtypeStruct((k, matrix.shape[1]), F32),
+            pltpu.VMEM(matrix.shape, matrix.dtype),
+        ],
+        in_specs=[vmem, pl.BlockSpec(memory_space=pltpu.MemorySpace.HBM)],
+        out_specs=[vmem, vmem],
+        scratch_shapes=[pltpu.VMEM((k, pieces_count * own), F32), pltpu.SemaphoreType.DMA((PARTS,))],
+        compiler_params=pltpu.CompilerParams(vmem_limit_bytes=16 << 20),
+        name="product1",
+    )(pieces, pltpu.with_memory_space_constraint(matrix, pltpu.MemorySpace.HBM))
 
 
 def step_kernel(normal, right_dim, last, *refs):
@@ -192,13 +224,11 @@
 def shards(initial, matrix):
     rows, columns = matrix.shape
     k = initial.shape[0]
-    matrix = pltpu.with_memory_space_constraint(matrix, pltpu.VMEM)
     copies = jnp.broadcast_to(initial, (lax.axis_size("col"), *initial.shape))
     pieces = lax.all_to_all(copies, "col", split_axis=0, concat_axis=0, tiled=True)
-    block = jnp.moveaxis(pieces, 0, 1).reshape(k, rows)
 
     estimates = jnp.zeros((k, LANES), F32)
-    (product,) = call(first_kernel, [(k, columns)], [], "product1", block, matrix)
+    product, matrix = first_product(pieces, matrix)
     terms = sum_over_row(product)
     (product,) = call(
         functools.partial(step_kernel, None, 1, False),

time: 93.2 us -> 88.3 us (0.947)
  waiting for transfers between devices: 28 us -> 23.5 us
  local copies, waits for them, and re-layouts: 4.59 us -> 0.78 us
  Pallas kernels: 9.78 us -> 12.5 us
    ppermute x24, waiting for transfers between devices: 28 us -> 23.5 us  [exchange(): return lax.ppermute(value, axis, pairs)]
    pallas_call x0 -> x1, Pallas kernels: none -> 4.01 us  [first_product(): pl.pallas_call(first_kernel, out_shape=[jax.ShapeDtypeStruct((k, matrix.s...]
    unnamed x4 -> x0, local copies, waits for them, and re-layouts: 3.68 us -> none
    pallas_call x6 -> x5, Pallas kernels: 9.78 us -> 8.46 us  [call(): pl.pallas_call(kernel, out_shape=[jax.ShapeDtypeStruct(s, F32) for s in s...]
where the time goes in v2:
time: 88.3 us; the launch traced here: 88.1 us
  starting transfers between devices  36 us (41%)
  waiting for transfers between devices  23.5 us (27%)
  blocking collectives  14.6 us (17%)
  Pallas kernels  12.5 us (14%)
    ppermute x24, starting transfers between devices, exchange(): return lax.ppermute(value, axis, pairs)  36 us
    ppermute x24, waiting for transfers between devices, exchange(): return lax.ppermute(value, axis, pairs)  23.5 us
    all_to_all x1, blocking collectives, shards(): lax.all_to_all(copies, 'col', split_axis=0, concat_axis=0, tiled=True)  14.6 us
    pallas_call x5, Pallas kernels, call(): pl.pallas_call(kernel, out_shape=[jax.ShapeDtypeStruct(s, F32) for s in s...  8.46 us
    pallas_call x1, Pallas kernels, first_product(): pl.pallas_call(first_kernel, out_shape=[jax.ShapeDtypeStruct((k, matrix.s...  4.01 us
  transfers between devices with their start and end apart: 24, of which 20 were waited for; matrix products, arithmetic and copies ran while one was open for 0% of the time, Pallas kernels for 0%

profile of v2, /device:TPU:0, one launch (start us, length us, event | category | flops | bytes accessed | tf_op | source)
XLA Modules:
  0.0 88.1 jit_solution(11853755399260301006)
XLA Ops:
  0.6 0.7 broadcast_in_dim.6
  1.3 14.6 %all_to_all.5.pieces_ref = bf16[16,8,192]{2,1,0:T(8,128)(2,1)S(1)} all-to-all(bf16[16,8,192]{2,1,0:T(8,128)(2,1)S(1)} %broadcast_in_dim.6), channel_id=1, replica_groups=mesh['row'=8,'col'=16] {'col'}, dimensions={0} | all-to-all | bytes 98304 | tf_op jit(solution)/shard_map/all_to_all | solution.py:228
  15.9 4.0 %product1.1 = (f32[8,1536]{1,0:T(8,128)S(1)}, bf16[3072,1536]{1,0:T(8,128)(2,1)S(1)}) custom-call(bf16[16,8,192]{2,1,0:T(8,128)(2,1)S(1)} %all_to_all.5.pieces_ref, bf16[3072,1536]{1,0:T(8,128)(2,1)} %matrix_ref.1), custom_call_target="tpu_custom_call" | custom-call | tf_op jit(solution)/shard_map/product1/pallas_call | solution.py:153
  20.0 1.2 %collective-permute-done = f32[8,1536]{1,0:T(8,128)S(1)} collective-permute-done((f32[8,1536]{1,0:T(8,128)S(1)}, f32[8,1536]{1,0:T(8,128)S(1)}, u32[]{:S(2)}, u32[]{:S(2)}) %collective-permute-start) | collective-permute-done | bytes 49184 | tf_op jit(solution)/shard_map/ppermute | solution.py:21
  21.2 4.0 %collective-permute-start.1 = (f32[8,1536]{1,0:T(8,128)S(1)}, f32[8,1536]{1,0:T(8,128)S(1)}, u32[]{:S(2)}, u32[]{:S(2)}) collective-permute-start(f32[8,1536]{1,0:T(8,128)S(1)} %add.32.refs_0_), channel_id=1, source_target_pairs={{0,64},{16,80},{32,96},{48,112},{64,0},{80,16},{96,32},{112,48},{1... | collective-permute-start | bytes 147464 | tf_op jit(solution)/shard_map/ppermute | solution.py:21
  25.2 1.0 %collective-permute-start.2 = (f32[8,1536]{1,0:T(8,128)S(1)}, f32[8,1536]{1,0:T(8,128)S(1)}, u32[]{:S(2)}, u32[]{:S(2)}) collective-permute-start(f32[8,1536]{1,0:T(8,128)S(1)} %add.32.refs_0_), channel_id=1, source_target_pairs={{0,32},{16,48},{32,64},{48,80},{64,96},{80,112},{96,0},{112,16},{1... | collective-permute-start | bytes 147464 | tf_op jit(solution)/shard_map/ppermute | solution.py:21
  26.2 2.2 %collective-permute-start.3 = (f32[8,1536]{1,0:T(8,128)S(1)}, f32[8,1536]{1,0:T(8,128)S(1)}, u32[]{:S(2)}, u32[]{:S(2)}) collective-permute-start(f32[8,1536]{1,0:T(8,128)S(1)} %add.32.refs_0_), channel_id=1, source_target_pairs={{0,96},{16,112},{32,0},{48,16},{64,32},{80,48},{96,64},{112,80},{1... | collective-permute-start | bytes 147464 | tf_op jit(solution)/shard_map/ppermute | solution.py:21
  28.4 2.1 %collective-permute-done.2.refs_2_ = f32[8,1536]{1,0:T(8,128)S(1)} collective-permute-done((f32[8,1536]{1,0:T(8,128)S(1)}, f32[8,1536]{1,0:T(8,128)S(1)}, u32[]{:S(2)}, u32[]{:S(2)}) %collective-permute-start.2) | collective-permute-done | bytes 49184 | tf_op jit(solution)/shard_map/ppermute | solution.py:21
  30.5 2.9 %product2.1 = f32[8,3200]{1,0:T(8,128)S(1)} custom-call(f32[8,1536]{1,0:T(8,128)S(1)} %add.32.refs_0_, f32[8,1536]{1,0:T(8,128)S(1)} %collective-permute-done.1.refs_1_, f32[8,1536]{1,0:T(8,128)S(1)} %collective-permute-done.2.refs_2_, f32[8,1536]{1,0:T(8,128)S(1)} %collective-permute-done.3.refs_3_, bf16[3072,1536]{1,0:T(8,128)(2,1)S(1)} %get-tuple-element.14.refs_4_.refs_5_), custom_call_target="tpu_custom_call" | custom-call | tf_op jit(solution)/shard_map/product2/pallas_call | solution.py:213
  33.4 1.4 %collective-permute-start.4 = (f32[8,3200]{1,0:T(8,128)S(1)}, f32[8,3200]{1,0:T(8,128)S(1)}, u32[]{:S(2)}, u32[]{:S(2)}) collective-permute-start(f32[8,3200]{1,0:T(8,128)S(1)} %product2.1), channel_id=1, source_target_pairs={{0,2},{1,3},{2,0},{3,1},{4,6},{5,7},{6,4},{7,5},{8,10},{9,11},{10,... | collective-permute-start | bytes 307208 | tf_op jit(solution)/shard_map/ppermute | solution.py:21
  34.8 0.7 collective-permute-start.5
  35.5 2.5 %collective-permute-start.6 = (f32[8,3200]{1,0:T(8,128)S(1)}, f32[8,3200]{1,0:T(8,128)S(1)}, u32[]{:S(2)}, u32[]{:S(2)}) collective-permute-start(f32[8,3200]{1,0:T(8,128)S(1)} %product2.1), channel_id=1, source_target_pairs={{0,3},{1,0},{2,1},{3,2},{4,7},{5,4},{6,5},{7,6},{8,11},{9,8},{10,9... | collective-permute-start | bytes 307208 | tf_op jit(solution)/shard_map/ppermute | solution.py:21
  38.0 1.6 %collective-permute-done.4 = f32[8,3200]{1,0:T(8,128)S(1)} collective-permute-done((f32[8,3200]{1,0:T(8,128)S(1)}, f32[8,3200]{1,0:T(8,128)S(1)}, u32[]{:S(2)}, u32[]{:S(2)}) %collective-permute-start.4) | collective-permute-done | bytes 102432 | tf_op jit(solution)/shard_map/ppermute | solution.py:21
  39.7 1.1 %collective-permute-done.5 = f32[8,3200]{1,0:T(8,128)S(1)} collective-permute-done((f32[8,3200]{1,0:T(8,128)S(1)}, f32[8,3200]{1,0:T(8,128)S(1)}, u32[]{:S(2)}, u32[]{:S(2)}) %collective-permute-start.5) | collective-permute-done | bytes 102432 | tf_op jit(solution)/shard_map/ppermute | solution.py:21
  40.8 1.2 %collective-permute-start.7 = (f32[8,3200]{1,0:T(8,128)S(1)}, f32[8,3200]{1,0:T(8,128)S(1)}, u32[]{:S(2)}, u32[]{:S(2)}) collective-permute-start(f32[8,3200]{1,0:T(8,128)S(1)} %add_add_fusion.1.refs_0_), channel_id=1, source_target_pairs={{0,8},{1,9},{2,10},{3,11},{4,12},{5,13},{6,14},{7,15},{8,0},{9,1},... | collective-permute-start | bytes 307208 | tf_op jit(solution)/shard_map/ppermute | solution.py:21
  42.1 0.8 collective-permute-start.8
  42.9 2.4 %collective-permute-start.9 = (f32[8,3200]{1,0:T(8,128)S(1)}, f32[8,3200]{1,0:T(8,128)S(1)}, u32[]{:S(2)}, u32[]{:S(2)}) collective-permute-start(f32[8,3200]{1,0:T(8,128)S(1)} %add_add_fusion.1.refs_0_), channel_id=1, source_target_pairs={{0,12},{1,13},{2,14},{3,15},{4,0},{5,1},{6,2},{7,3},{8,4},{9,5},{1... | collective-permute-start | bytes 307208 | tf_op jit(solution)/shard_map/ppermute | solution.py:21
  45.3 1.8 %collective-permute-done.7.refs_1_ = f32[8,3200]{1,0:T(8,128)S(1)} collective-permute-done((f32[8,3200]{1,0:T(8,128)S(1)}, f32[8,3200]{1,0:T(8,128)S(1)}, u32[]{:S(2)}, u32[]{:S(2)}) %collective-permute-start.7) | collective-permute-done | bytes 102432 | tf_op jit(solution)/shard_map/ppermute | solution.py:21
  47.1 1.1 %collective-permute-done.8.refs_2_ = f32[8,3200]{1,0:T(8,128)S(1)} collective-permute-done((f32[8,3200]{1,0:T(8,128)S(1)}, f32[8,3200]{1,0:T(8,128)S(1)}, u32[]{:S(2)}, u32[]{:S(2)}) %collective-permute-start.8) | collective-permute-done | bytes 102432 | tf_op jit(solution)/shard_map/ppermute | solution.py:21
  48.2 1.6 %product3.1 = (f32[8,1664]{1,0:T(8,128)S(1)}, f32[8,128]{1,0:T(8,128)S(1)}) custom-call(f32[8,3200]{1,0:T(8,128)S(1)} %add_add_fusion.1.refs_0_, f32[8,3200]{1,0:T(8,128)S(1)} %collective-permute-done.7.refs_1_, f32[8,3200]{1,0:T(8,128)S(1)} %collective-permute-done.8.refs_2_, f32[8,3200]{1,0:T(8,128)S(1)} %collective-permute-done.9.refs_3_, ...), custom_call_target="tpu_custom_call" | custom-call | tf_op jit(solution)/shard_map/product3/pallas_call | solution.py:213
  49.8 1.2 %collective-permute-done.10 = f32[8,1664]{1,0:T(8,128)S(1)} collective-permute-done((f32[8,1664]{1,0:T(8,128)S(1)}, f32[8,1664]{1,0:T(8,128)S(1)}, u32[]{:S(2)}, u32[]{:S(2)}) %collective-permute-start.10) | collective-permute-done | bytes 53280 | tf_op jit(solution)/shard_map/ppermute | solution.py:21
  51.0 1.7 %collective-permute-start.11 = (f32[8,1664]{1,0:T(8,128)S(1)}, f32[8,1664]{1,0:T(8,128)S(1)}, u32[]{:S(2)}, u32[]{:S(2)}) collective-permute-start(f32[8,1664]{1,0:T(8,128)S(1)} %add.36.refs_0_), channel_id=1, source_target_pairs={{0,64},{16,80},{32,96},{48,112},{64,0},{80,16},{96,32},{112,48},{1... | collective-permute-start | bytes 159752 | tf_op jit(solution)/shard_map/ppermute | solution.py:21
  52.8 2.5 %collective-permute-start.12 = (f32[8,1664]{1,0:T(8,128)S(1)}, f32[8,1664]{1,0:T(8,128)S(1)}, u32[]{:S(2)}, u32[]{:S(2)}) collective-permute-start(f32[8,1664]{1,0:T(8,128)S(1)} %add.36.refs_0_), channel_id=1, source_target_pairs={{0,32},{16,48},{32,64},{48,80},{64,96},{80,112},{96,0},{112,16},{1... | collective-permute-start | bytes 159752 | tf_op jit(solution)/shard_map/ppermute | solution.py:21
  55.2 0.8 collective-permute-start.13
  56.0 1.0 %collective-permute-done.11.refs_1_ = f32[8,1664]{1,0:T(8,128)S(1)} collective-permute-done((f32[8,1664]{1,0:T(8,128)S(1)}, f32[8,1664]{1,0:T(8,128)S(1)}, u32[]{:S(2)}, u32[]{:S(2)}) %collective-permute-start.11) | collective-permute-done | bytes 53280 | tf_op jit(solution)/shard_map/ppermute | solution.py:21
  57.0 1.1 %collective-permute-done.12.refs_2_ = f32[8,1664]{1,0:T(8,128)S(1)} collective-permute-done((f32[8,1664]{1,0:T(8,128)S(1)}, f32[8,1664]{1,0:T(8,128)S(1)}, u32[]{:S(2)}, u32[]{:S(2)}) %collective-permute-start.12) | collective-permute-done | bytes 53280 | tf_op jit(solution)/shard_map/ppermute | solution.py:21
  58.1 1.2 %collective-permute-done.13.refs_3_ = f32[8,1664]{1,0:T(8,128)S(1)} collective-permute-done((f32[8,1664]{1,0:T(8,128)S(1)}, f32[8,1664]{1,0:T(8,128)S(1)}, u32[]{:S(2)}, u32[]{:S(2)}) %collective-permute-start.13) | collective-permute-done | bytes 53280 | tf_op jit(solution)/shard_map/ppermute | solution.py:21
  59.3 2.7 %product4.1 = (f32[8,3200]{1,0:T(8,128)S(1)}, f32[8,128]{1,0:T(8,128)S(1)}) custom-call(f32[8,1664]{1,0:T(8,128)S(1)} %add.36.refs_0_, f32[8,1664]{1,0:T(8,128)S(1)} %collective-permute-done.11.refs_1_, f32[8,1664]{1,0:T(8,128)S(1)} %collective-permute-done.12.refs_2_, f32[8,1664]{1,0:T(8,128)S(1)} %collective-permute-done.13.refs_3_, ...), custom_call_target="tpu_custom_call" | custom-call | tf_op jit(solution)/shard_map/product4/pallas_call | solution.py:213
  62.1 2.1 %collective-permute-start.14 = (f32[8,3200]{1,0:T(8,128)S(1)}, f32[8,3200]{1,0:T(8,128)S(1)}, u32[]{:S(2)}, u32[]{:S(2)}) collective-permute-start(f32[8,3200]{1,0:T(8,128)S(1)} %get-tuple-element.17), channel_id=1, source_target_pairs={{0,2},{1,3},{2,0},{3,1},{4,6},{5,7},{6,4},{7,5},{8,10},{9,11},{10,... | collective-permute-start | bytes 307208 | tf_op jit(solution)/shard_map/ppermute | solution.py:21
  64.2 1.9 %collective-permute-start.15 = (f32[8,3200]{1,0:T(8,128)S(1)}, f32[8,3200]{1,0:T(8,128)S(1)}, u32[]{:S(2)}, u32[]{:S(2)}) collective-permute-start(f32[8,3200]{1,0:T(8,128)S(1)} %get-tuple-element.17), channel_id=1, source_target_pairs={{0,1},{1,2},{2,3},{3,0},{4,5},{5,6},{6,7},{7,4},{8,9},{9,10},{10,1... | collective-permute-start | bytes 307208 | tf_op jit(solution)/shard_map/ppermute | solution.py:21
  66.1 1.3 %collective-permute-start.16 = (f32[8,3200]{1,0:T(8,128)S(1)}, f32[8,3200]{1,0:T(8,128)S(1)}, u32[]{:S(2)}, u32[]{:S(2)}) collective-permute-start(f32[8,3200]{1,0:T(8,128)S(1)} %get-tuple-element.17), channel_id=1, source_target_pairs={{0,3},{1,0},{2,1},{3,2},{4,7},{5,4},{6,5},{7,6},{8,11},{9,8},{10,9... | collective-permute-start | bytes 307208 | tf_op jit(solution)/shard_map/ppermute | solution.py:21
  67.4 1.0 %collective-permute-done.14 = f32[8,3200]{1,0:T(8,128)S(1)} collective-permute-done((f32[8,3200]{1,0:T(8,128)S(1)}, f32[8,3200]{1,0:T(8,128)S(1)}, u32[]{:S(2)}, u32[]{:S(2)}) %collective-permute-start.14) | collective-permute-done | bytes 102432 | tf_op jit(solution)/shard_map/ppermute | solution.py:21
  68.4 1.7 %collective-permute-done.15 = f32[8,3200]{1,0:T(8,128)S(1)} collective-permute-done((f32[8,3200]{1,0:T(8,128)S(1)}, f32[8,3200]{1,0:T(8,128)S(1)}, u32[]{:S(2)}, u32[]{:S(2)}) %collective-permute-start.15) | collective-permute-done | bytes 102432 | tf_op jit(solution)/shard_map/ppermute | solution.py:21
  70.1 0.7 collective-permute-done.16
  70.8 2.2 %collective-permute-start.17 = (f32[8,3200]{1,0:T(8,128)S(1)}, f32[8,3200]{1,0:T(8,128)S(1)}, u32[]{:S(2)}, u32[]{:S(2)}) collective-permute-start(f32[8,3200]{1,0:T(8,128)S(1)} %add_add_fusion.refs_0_), channel_id=1, source_target_pairs={{0,8},{1,9},{2,10},{3,11},{4,12},{5,13},{6,14},{7,15},{8,0},{9,1},... | collective-permute-start | bytes 307208 | tf_op jit(solution)/shard_map/ppermute | solution.py:21
  73.0 1.8 %collective-permute-start.18 = (f32[8,3200]{1,0:T(8,128)S(1)}, f32[8,3200]{1,0:T(8,128)S(1)}, u32[]{:S(2)}, u32[]{:S(2)}) collective-permute-start(f32[8,3200]{1,0:T(8,128)S(1)} %add_add_fusion.refs_0_), channel_id=1, source_target_pairs={{0,4},{1,5},{2,6},{3,7},{4,8},{5,9},{6,10},{7,11},{8,12},{9,13},{1... | collective-permute-start | bytes 307208 | tf_op jit(solution)/shard_map/ppermute | solution.py:21
  74.8 1.4 %collective-permute-start.19 = (f32[8,3200]{1,0:T(8,128)S(1)}, f32[8,3200]{1,0:T(8,128)S(1)}, u32[]{:S(2)}, u32[]{:S(2)}) collective-permute-start(f32[8,3200]{1,0:T(8,128)S(1)} %add_add_fusion.refs_0_), channel_id=1, source_target_pairs={{0,12},{1,13},{2,14},{3,15},{4,0},{5,1},{6,2},{7,3},{8,4},{9,5},{1... | collective-permute-start | bytes 307208 | tf_op jit(solution)/shard_map/ppermute | solution.py:21
  76.2 0.8 collective-permute-done.17.refs_1_
  77.0 1.8 %collective-permute-done.18.refs_2_ = f32[8,3200]{1,0:T(8,128)S(1)} collective-permute-done((f32[8,3200]{1,0:T(8,128)S(1)}, f32[8,3200]{1,0:T(8,128)S(1)}, u32[]{:S(2)}, u32[]{:S(2)}) %collective-permute-start.18) | collective-permute-done | bytes 102432 | tf_op jit(solution)/shard_map/ppermute | solution.py:21
  78.8 0.6 collective-permute-done.19.refs_3_
  79.4 0.4 last_gram.1
  79.9 1.2 %collective-permute-done.20 = f32[8,128]{1,0:T(8,128)S(1)} collective-permute-done((f32[8,128]{1,0:T(8,128)S(1)}, f32[8,128]{1,0:T(8,128)S(1)}, u32[]{:S(2)}, u32[]{:S(2)}) %collective-permute-start.20) | collective-permute-done | bytes 4128 | tf_op jit(solution)/shard_map/ppermute | solution.py:21
  81.0 0.7 collective-permute-start.21
  81.7 2.0 %collective-permute-start.22 = (f32[8,128]{1,0:T(8,128)S(1)}, f32[8,128]{1,0:T(8,128)S(1)}, u32[]{:S(2)}, u32[]{:S(2)}) collective-permute-start(f32[8,128]{1,0:T(8,128)S(1)} %add.40.a_ref), channel_id=1, source_target_pairs={{0,32},{16,48},{32,64},{48,80},{64,96},{80,112},{96,0},{112,16},{1... | collective-permute-start | bytes 12296 | tf_op jit(solution)/shard_map/ppermute | solution.py:21
  83.7 1.2 %collective-permute-start.23 = (f32[8,128]{1,0:T(8,128)S(1)}, f32[8,128]{1,0:T(8,128)S(1)}, u32[]{:S(2)}, u32[]{:S(2)}) collective-permute-start(f32[8,128]{1,0:T(8,128)S(1)} %add.40.a_ref), channel_id=1, source_target_pairs={{0,96},{16,112},{32,0},{48,16},{64,32},{80,48},{96,64},{112,80},{1... | collective-permute-start | bytes 12296 | tf_op jit(solution)/shard_map/ppermute | solution.py:21
  85.0 1.1 %collective-permute-done.21.b_ref = f32[8,128]{1,0:T(8,128)S(1)} collective-permute-done((f32[8,128]{1,0:T(8,128)S(1)}, f32[8,128]{1,0:T(8,128)S(1)}, u32[]{:S(2)}, u32[]{:S(2)}) %collective-permute-start.21) | collective-permute-done | bytes 4128 | tf_op jit(solution)/shard_map/ppermute | solution.py:21
  86.5 0.8 collective-permute-done.23.d_ref
  87.3 0.8 final.1
  (16 shorter events, 0.7 us)
Async XLA Ops:
  19.9 1.3 %collective-permute-start = (f32[8,1536]{1,0:T(8,128)S(1)}, f32[8,1536]{1,0:T(8,128)S(1)}, u32[]{:S(2)}, u32[]{:S(2)}) collective-permute-start(f32[8,1536]{1,0:T(8,128)S(1)} %get-tuple-element.13), channel_id=1, source_target_pairs={{0,16},{16,0},{32,48},{48,32},{64,80},{80,64},{96,112},{112,96},{1... | collective-permute-start | bytes 147464 | tf_op jit(solution)/shard_map/ppermute | solution.py:21
  21.2 7.2 %collective-permute-start.1 = (f32[8,1536]{1,0:T(8,128)S(1)}, f32[8,1536]{1,0:T(8,128)S(1)}, u32[]{:S(2)}, u32[]{:S(2)}) collective-permute-start(f32[8,1536]{1,0:T(8,128)S(1)} %add.32.refs_0_), channel_id=1, source_target_pairs={{0,64},{16,80},{32,96},{48,112},{64,0},{80,16},{96,32},{112,48},{1... | collective-permute-start | bytes 147464 | tf_op jit(solution)/shard_map/ppermute | solution.py:21
  25.2 5.3 %collective-permute-start.2 = (f32[8,1536]{1,0:T(8,128)S(1)}, f32[8,1536]{1,0:T(8,128)S(1)}, u32[]{:S(2)}, u32[]{:S(2)}) collective-permute-start(f32[8,1536]{1,0:T(8,128)S(1)} %add.32.refs_0_), channel_id=1, source_target_pairs={{0,32},{16,48},{32,64},{48,80},{64,96},{80,112},{96,0},{112,16},{1... | collective-permute-start | bytes 147464 | tf_op jit(solution)/shard_map/ppermute | solution.py:21
  26.2 4.3 %collective-permute-start.3 = (f32[8,1536]{1,0:T(8,128)S(1)}, f32[8,1536]{1,0:T(8,128)S(1)}, u32[]{:S(2)}, u32[]{:S(2)}) collective-permute-start(f32[8,1536]{1,0:T(8,128)S(1)} %add.32.refs_0_), channel_id=1, source_target_pairs={{0,96},{16,112},{32,0},{48,16},{64,32},{80,48},{96,64},{112,80},{1... | collective-permute-start | bytes 147464 | tf_op jit(solution)/shard_map/ppermute | solution.py:21
  33.4 6.2 %collective-permute-start.4 = (f32[8,3200]{1,0:T(8,128)S(1)}, f32[8,3200]{1,0:T(8,128)S(1)}, u32[]{:S(2)}, u32[]{:S(2)}) collective-permute-start(f32[8,3200]{1,0:T(8,128)S(1)} %product2.1), channel_id=1, source_target_pairs={{0,2},{1,3},{2,0},{3,1},{4,6},{5,7},{6,4},{7,5},{8,10},{9,11},{10,... | collective-permute-start | bytes 307208 | tf_op jit(solution)/shard_map/ppermute | solution.py:21
  34.8 6.0 %collective-permute-start.5 = (f32[8,3200]{1,0:T(8,128)S(1)}, f32[8,3200]{1,0:T(8,128)S(1)}, u32[]{:S(2)}, u32[]{:S(2)}) collective-permute-start(f32[8,3200]{1,0:T(8,128)S(1)} %product2.1), channel_id=1, source_target_pairs={{0,1},{1,2},{2,3},{3,0},{4,5},{5,6},{6,7},{7,4},{8,9},{9,10},{10,1... | collective-permute-start | bytes 307208 | tf_op jit(solution)/shard_map/ppermute | solution.py:21
  35.5 5.2 %collective-permute-start.6 = (f32[8,3200]{1,0:T(8,128)S(1)}, f32[8,3200]{1,0:T(8,128)S(1)}, u32[]{:S(2)}, u32[]{:S(2)}) collective-permute-start(f32[8,3200]{1,0:T(8,128)S(1)} %product2.1), channel_id=1, source_target_pairs={{0,3},{1,0},{2,1},{3,2},{4,7},{5,4},{6,5},{7,6},{8,11},{9,8},{10,9... | collective-permute-start | bytes 307208 | tf_op jit(solution)/shard_map/ppermute | solution.py:21
  40.8 6.3 %collective-permute-start.7 = (f32[8,3200]{1,0:T(8,128)S(1)}, f32[8,3200]{1,0:T(8,128)S(1)}, u32[]{:S(2)}, u32[]{:S(2)}) collective-permute-start(f32[8,3200]{1,0:T(8,128)S(1)} %add_add_fusion.1.refs_0_), channel_id=1, source_target_pairs={{0,8},{1,9},{2,10},{3,11},{4,12},{5,13},{6,14},{7,15},{8,0},{9,1},... | collective-permute-start | bytes 307208 | tf_op jit(solution)/shard_map/ppermute | solution.py:21
  42.1 6.1 %collective-permute-start.8 = (f32[8,3200]{1,0:T(8,128)S(1)}, f32[8,3200]{1,0:T(8,128)S(1)}, u32[]{:S(2)}, u32[]{:S(2)}) collective-permute-start(f32[8,3200]{1,0:T(8,128)S(1)} %add_add_fusion.1.refs_0_), channel_id=1, source_target_pairs={{0,4},{1,5},{2,6},{3,7},{4,8},{5,9},{6,10},{7,11},{8,12},{9,13},{1... | collective-permute-start | bytes 307208 | tf_op jit(solution)/shard_map/ppermute | solution.py:21
  42.9 5.3 %collective-permute-start.9 = (f32[8,3200]{1,0:T(8,128)S(1)}, f32[8,3200]{1,0:T(8,128)S(1)}, u32[]{:S(2)}, u32[]{:S(2)}) collective-permute-start(f32[8,3200]{1,0:T(8,128)S(1)} %add_add_fusion.1.refs_0_), channel_id=1, source_target_pairs={{0,12},{1,13},{2,14},{3,15},{4,0},{5,1},{6,2},{7,3},{8,4},{9,5},{1... | collective-permute-start | bytes 307208 | tf_op jit(solution)/shard_map/ppermute | solution.py:21
  49.8 1.2 %collective-permute-start.10 = (f32[8,1664]{1,0:T(8,128)S(1)}, f32[8,1664]{1,0:T(8,128)S(1)}, u32[]{:S(2)}, u32[]{:S(2)}) collective-permute-start(f32[8,1664]{1,0:T(8,128)S(1)} %get-tuple-element.15), channel_id=1, source_target_pairs={{0,16},{16,0},{32,48},{48,32},{64,80},{80,64},{96,112},{112,96},{1... | collective-permute-start | bytes 159752 | tf_op jit(solution)/shard_map/ppermute | solution.py:21
  51.0 6.0 %collective-permute-start.11 = (f32[8,1664]{1,0:T(8,128)S(1)}, f32[8,1664]{1,0:T(8,128)S(1)}, u32[]{:S(2)}, u32[]{:S(2)}) collective-permute-start(f32[8,1664]{1,0:T(8,128)S(1)} %add.36.refs_0_), channel_id=1, source_target_pairs={{0,64},{16,80},{32,96},{48,112},{64,0},{80,16},{96,32},{112,48},{1... | collective-permute-start | bytes 159752 | tf_op jit(solution)/shard_map/ppermute | solution.py:21
  52.8 5.3 %collective-permute-start.12 = (f32[8,1664]{1,0:T(8,128)S(1)}, f32[8,1664]{1,0:T(8,128)S(1)}, u32[]{:S(2)}, u32[]{:S(2)}) collective-permute-start(f32[8,1664]{1,0:T(8,128)S(1)} %add.36.refs_0_), channel_id=1, source_target_pairs={{0,32},{16,48},{32,64},{48,80},{64,96},{80,112},{96,0},{112,16},{1... | collective-permute-start | bytes 159752 | tf_op jit(solution)/shard_map/ppermute | solution.py:21
  55.2 4.1 %collective-permute-start.13 = (f32[8,1664]{1,0:T(8,128)S(1)}, f32[8,1664]{1,0:T(8,128)S(1)}, u32[]{:S(2)}, u32[]{:S(2)}) collective-permute-start(f32[8,1664]{1,0:T(8,128)S(1)} %add.36.refs_0_), channel_id=1, source_target_pairs={{0,96},{16,112},{32,0},{48,16},{64,32},{80,48},{96,64},{112,80},{1... | collective-permute-start | bytes 159752 | tf_op jit(solution)/shard_map/ppermute | solution.py:21
  62.1 6.3 %collective-permute-start.14 = (f32[8,3200]{1,0:T(8,128)S(1)}, f32[8,3200]{1,0:T(8,128)S(1)}, u32[]{:S(2)}, u32[]{:S(2)}) collective-permute-start(f32[8,3200]{1,0:T(8,128)S(1)} %get-tuple-element.17), channel_id=1, source_target_pairs={{0,2},{1,3},{2,0},{3,1},{4,6},{5,7},{6,4},{7,5},{8,10},{9,11},{10,... | collective-permute-start | bytes 307208 | tf_op jit(solution)/shard_map/ppermute | solution.py:21
  64.2 5.9 %collective-permute-start.15 = (f32[8,3200]{1,0:T(8,128)S(1)}, f32[8,3200]{1,0:T(8,128)S(1)}, u32[]{:S(2)}, u32[]{:S(2)}) collective-permute-start(f32[8,3200]{1,0:T(8,128)S(1)} %get-tuple-element.17), channel_id=1, source_target_pairs={{0,1},{1,2},{2,3},{3,0},{4,5},{5,6},{6,7},{7,4},{8,9},{9,10},{10,1... | collective-permute-start | bytes 307208 | tf_op jit(solution)/shard_map/ppermute | solution.py:21
  66.1 4.7 %collective-permute-start.16 = (f32[8,3200]{1,0:T(8,128)S(1)}, f32[8,3200]{1,0:T(8,128)S(1)}, u32[]{:S(2)}, u32[]{:S(2)}) collective-permute-start(f32[8,3200]{1,0:T(8,128)S(1)} %get-tuple-element.17), channel_id=1, source_target_pairs={{0,3},{1,0},{2,1},{3,2},{4,7},{5,4},{6,5},{7,6},{8,11},{9,8},{10,9... | collective-permute-start | bytes 307208 | tf_op jit(solution)/shard_map/ppermute | solution.py:21
  70.8 6.2 %collective-permute-start.17 = (f32[8,3200]{1,0:T(8,128)S(1)}, f32[8,3200]{1,0:T(8,128)S(1)}, u32[]{:S(2)}, u32[]{:S(2)}) collective-permute-start(f32[8,3200]{1,0:T(8,128)S(1)} %add_add_fusion.refs_0_), channel_id=1, source_target_pairs={{0,8},{1,9},{2,10},{3,11},{4,12},{5,13},{6,14},{7,15},{8,0},{9,1},... | collective-permute-start | bytes 307208 | tf_op jit(solution)/shard_map/ppermute | solution.py:21
  73.0 5.9 %collective-permute-start.18 = (f32[8,3200]{1,0:T(8,128)S(1)}, f32[8,3200]{1,0:T(8,128)S(1)}, u32[]{:S(2)}, u32[]{:S(2)}) collective-permute-start(f32[8,3200]{1,0:T(8,128)S(1)} %add_add_fusion.refs_0_), channel_id=1, source_target_pairs={{0,4},{1,5},{2,6},{3,7},{4,8},{5,9},{6,10},{7,11},{8,12},{9,13},{1... | collective-permute-start | bytes 307208 | tf_op jit(solution)/shard_map/ppermute | solution.py:21
  74.8 4.7 %collective-permute-start.19 = (f32[8,3200]{1,0:T(8,128)S(1)}, f32[8,3200]{1,0:T(8,128)S(1)}, u32[]{:S(2)}, u32[]{:S(2)}) collective-permute-start(f32[8,3200]{1,0:T(8,128)S(1)} %add_add_fusion.refs_0_), channel_id=1, source_target_pairs={{0,12},{1,13},{2,14},{3,15},{4,0},{5,1},{6,2},{7,3},{8,4},{9,5},{1... | collective-permute-start | bytes 307208 | tf_op jit(solution)/shard_map/ppermute | solution.py:21
  79.9 1.2 %collective-permute-start.20 = (f32[8,128]{1,0:T(8,128)S(1)}, f32[8,128]{1,0:T(8,128)S(1)}, u32[]{:S(2)}, u32[]{:S(2)}) collective-permute-start(f32[8,128]{1,0:T(8,128)S(1)} %get-tuple-element.19), channel_id=1, source_target_pairs={{0,16},{16,0},{32,48},{48,32},{64,80},{80,64},{96,112},{112,96},{1... | collective-permute-start | bytes 12296 | tf_op jit(solution)/shard_map/ppermute | solution.py:21
  81.0 5.1 %collective-permute-start.21 = (f32[8,128]{1,0:T(8,128)S(1)}, f32[8,128]{1,0:T(8,128)S(1)}, u32[]{:S(2)}, u32[]{:S(2)}) collective-permute-start(f32[8,128]{1,0:T(8,128)S(1)} %add.40.a_ref), channel_id=1, source_target_pairs={{0,64},{16,80},{32,96},{48,112},{64,0},{80,16},{96,32},{112,48},{1... | collective-permute-start | bytes 12296 | tf_op jit(solution)/shard_map/ppermute | solution.py:21
  81.7 4.8 %collective-permute-start.22 = (f32[8,128]{1,0:T(8,128)S(1)}, f32[8,128]{1,0:T(8,128)S(1)}, u32[]{:S(2)}, u32[]{:S(2)}) collective-permute-start(f32[8,128]{1,0:T(8,128)S(1)} %add.40.a_ref), channel_id=1, source_target_pairs={{0,32},{16,48},{32,64},{48,80},{64,96},{80,112},{96,0},{112,16},{1... | collective-permute-start | bytes 12296 | tf_op jit(solution)/shard_map/ppermute | solution.py:21
  83.7 3.6 %collective-permute-start.23 = (f32[8,128]{1,0:T(8,128)S(1)}, f32[8,128]{1,0:T(8,128)S(1)}, u32[]{:S(2)}, u32[]{:S(2)}) collective-permute-start(f32[8,128]{1,0:T(8,128)S(1)} %add.40.a_ref), channel_id=1, source_target_pairs={{0,96},{16,112},{32,0},{48,16},{64,32},{80,48},{96,64},{112,80},{1... | collective-permute-start | bytes 12296 | tf_op jit(solution)/shard_map/ppermute | solution.py:21

commit v3 on v2

--- a/solution.py
+++ b/solution.py
@@ -51,6 +51,23 @@
 
 def sum_over_row(value):
     return row_block(value + exchange(value, "row", lambda i: i ^ 1))
+
+
+def gathered_over_col(value, held):
+    def turned(step_y, step_x):
+        return lambda i: (i // 4 - step_y) % 4 * 4 + (i % 4 - step_x) % 4
+    far, up, down = (exchange(value, "col", turned(0, n)) for n in (2, 1, 3))
+    vmem = pl.BlockSpec(memory_space=pltpu.VMEM)
+    line = pl.pallas_call(
+        line_kernel,
+        out_shape=jax.ShapeDtypeStruct((4, *value.shape), value.dtype),
+        in_specs=[vmem] * 5,
+        out_specs=vmem,
+        compiler_params=pltpu.CompilerParams(vmem_limit_bytes=1 << 20),
+        name="line",
+    )(value, far, up, down, held)
+    far, up, down = (exchange(line, "col", turned(n, 0)) for n in (2, 1, 3))
+    return (line, far, up, down)
 
 
 def chunks_of(refs, width):
@@ -115,60 +132,80 @@
     return gram
 
 
-def product_into(out_ref, terms_ref, matrix_ref, right_dim):
+def contract_rows(left, matrix_refs):
+    out, at = None, 0
+    for ref in matrix_refs:
+        part = contract(left[:, at:at + ref.shape[0]], ref[...], 0)
+        out = part if out is None else out + part
+        at += ref.shape[0]
+    return out
+
+
+def product_into(out_ref, terms_ref, matrix_refs, right_dim):
     left = terms_ref[...]
     if right_dim == 0:
-        out_ref[:, :matrix_ref.shape[1]] = rows_added(contract(left, matrix_ref[...], 0))
-    else:
-        step = 512
-        for n in range(0, matrix_ref.shape[0], step):
-            out_ref[:, n:n + step] = rows_added(contract(left, matrix_ref[n:n + step, :], 1))
-
-
-PARTS = 12
-
-
-def first_kernel(pieces_ref, matrix_ref, out_ref, held_ref, block_ref, arrived):
-    size = matrix_ref.shape[0] // PARTS
-    own = pieces_ref.shape[2]
+        out_ref[:, :matrix_refs[0].shape[1]] = rows_added(contract_rows(left, matrix_refs))
+        return
+    step, at = 512, 0
+    for ref in matrix_refs:
+        for n in range(0, ref.shape[0], step):
+            out_ref[:, at:at + step] = rows_added(contract(left, ref[n:n + step, :], 1))
+            at += step
+
+
+def line_kernel(a_ref, c_ref, b_ref, d_ref, held_ref, line_ref):
+    del held_ref
+    for n, ref in enumerate((a_ref, b_ref, c_ref, d_ref)):
+        line_ref[n] = ref[...]
+
+
+def first_kernel(a_ref, c_ref, b_ref, d_ref, *refs):
+    *matrix_refs, out_ref, block_ref = refs
+    own = a_ref.shape[2]
+    place = lax.axis_index("col")
+    for mine in range(16):
+        @pl.when(place == mine)
+        def _():
+            for b, ref in enumerate((a_ref, b_ref, c_ref, d_ref)):
+                for a in range(4):
+                    n = (mine // 4 + b) % 4 * 4 + (mine % 4 + a) % 4
+                    block_ref[:, n * own:(n + 1) * own] = ref[a].astype(F32)
+    out_ref[...] = contract_rows(block_ref[...].astype(BF16), matrix_refs)
+
+
+PARTS = 6
+
+
+def load_kernel(start, matrix_ref, held_ref, arrived):
+    size = held_ref.shape[0] // PARTS
     copies = []
     for n in range(PARTS):
-        part = pl.ds(n * size, size)
-        copies.append(pltpu.make_async_copy(matrix_ref.at[part], held_ref.at[part], arrived.at[n]))
+        source = matrix_ref.at[pl.ds(start + n * size, size)]
+        copies.append(pltpu.make_async_copy(source, held_ref.at[pl.ds(n * size, size)], arrived.at[n]))
         copies[-1].start()
-    for n in range(pieces_ref.shape[0]):
-        block_ref[:, n * own:(n + 1) * own] = pieces_ref[n].astype(F32)
-    product = None
-    for n, copy in enumerate(copies):
+    for copy in copies:
         copy.wait()
-        part = slice(n * size, (n + 1) * size)
-        term = contract(block_ref[:, part].astype(BF16), held_ref[part, :], 0)
-        product = term if product is None else product + term
-    out_ref[...] = product
-
-
-def first_product(pieces, matrix):
-    pieces_count, k, own = pieces.shape
-    vmem = pl.BlockSpec(memory_space=pltpu.VMEM)
+
+
+def held_half(matrix, half):
+    rows, columns = matrix.shape
     return pl.pallas_call(
-        first_kernel,
-        out_shape=[
-            jax.ShapeDtypeStruct((k, matrix.shape[1]), F32),
-            pltpu.VMEM(matrix.shape, matrix.dtype),
-        ],
-        in_specs=[vmem, pl.BlockSpec(memory_space=pltpu.MemorySpace.HBM)],
-        out_specs=[vmem, vmem],
-        scratch_shapes=[pltpu.VMEM((k, pieces_count * own), F32), pltpu.SemaphoreType.DMA((PARTS,))],
+        functools.partial(load_kernel, half * (rows // 2)),
+        out_shape=pltpu.VMEM((rows // 2, columns), matrix.dtype),
+        in_specs=[pl.BlockSpec(memory_space=pltpu.MemorySpace.HBM)],
+        out_specs=pl.BlockSpec(memory_space=pltpu.VMEM),
+        scratch_shapes=[pltpu.SemaphoreType.DMA((PARTS,))],
+        cost_estimate=pl.CostEstimate(flops=0, bytes_accessed=matrix.size, transcendentals=0),
         compiler_params=pltpu.CompilerParams(vmem_limit_bytes=16 << 20),
-        name="product1",
-    )(pieces, pltpu.with_memory_space_constraint(matrix, pltpu.MemorySpace.HBM))
+        name=f"held_half{half}",
+    )(matrix)
 
 
 def step_kernel(normal, right_dim, last, *refs):
     refs = list(refs)
     terms = [refs.pop(0) for _ in range(4)]
     estimates_ref = refs.pop(0) if normal is not None else None
-    matrix_ref = None if last else refs.pop(0)
+    matrix_refs = None if last else [refs.pop(0) for _ in range(2)]
     width = terms[0].shape[1]
     if normal is None:
         out_ref, split_ref = refs
@@ -190,7 +227,7 @@
             block_ref[:, n * LANES:(n + 1) * LANES] = chunk
         at = 0
     else:
-        product_into(out_ref, split_ref, matrix_ref, right_dim)
+        product_into(out_ref, split_ref, matrix_refs, right_dim)
         at = out_ref.shape[1] - LANES
     out_ref[:, at:] = jnp.zeros((8, LANES), F32)
     out_ref[:, at:at + 8] = gram
@@ -215,7 +252,7 @@
         out_shape=[jax.ShapeDtypeStruct(s, F32) for s in shapes],
         in_specs=[vmem] * len(args),
         out_specs=[vmem] * len(shapes),
-        scratch_shapes=[pltpu.VMEM(s, BF16) for s in scratch],
+        scratch_shapes=[pltpu.VMEM(s, t) for s, t in scratch],
         compiler_params=pltpu.CompilerParams(vmem_limit_bytes=16 << 20),
         name=name,
     )(*args)
@@ -224,27 +261,29 @@
 def shards(initial, matrix):
     rows, columns = matrix.shape
     k = initial.shape[0]
-    copies = jnp.broadcast_to(initial, (lax.axis_size("col"), *initial.shape))
-    pieces = lax.all_to_all(copies, "col", split_axis=0, concat_axis=0, tiled=True)
+    matrix = pltpu.with_memory_space_constraint(matrix, pltpu.MemorySpace.HBM)
+    halves = [held_half(matrix, n) for n in range(2)]
+    pieces = gathered_over_col(initial, halves[0])
 
     estimates = jnp.zeros((k, LANES), F32)
-    product, matrix = first_product(pieces, matrix)
+    (product,) = call(
+        first_kernel, [(k, columns)], [((k, rows), F32)], "product1", *pieces, *halves)
     terms = sum_over_row(product)
     (product,) = call(
         functools.partial(step_kernel, None, 1, False),
-        [(k, rows + LANES)], [(24, columns)], "product2", *terms, matrix)
+        [(k, rows + LANES)], [((24, columns), BF16)], "product2", *terms, *halves)
     terms = sum_over_col(product)
     product, estimates = call(
         functools.partial(step_kernel, 0, 0, False),
-        [(k, columns + LANES), (k, LANES)], [(16, rows)], "product3", *terms, estimates, matrix)
+        [(k, columns + LANES), (k, LANES)], [((16, rows), BF16)], "product3", *terms, estimates, *halves)
     terms = sum_over_row(product)
     product, estimates = call(
         functools.partial(step_kernel, 1, 1, False),
-        [(k, rows + LANES), (k, LANES)], [(16, columns)], "product4", *terms, estimates, matrix)
+        [(k, rows + LANES), (k, LANES)], [((16, columns), BF16)], "product4", *terms, estimates, *halves)
     terms = sum_over_col(product)
     gram, block, estimates = call(
         functools.partial(step_kernel, 2, None, True),
-        [(k, LANES), (k, rows), (k, LANES)], [(16, rows)], "last_gram", *terms, estimates)
+        [(k, LANES), (k, rows), (k, LANES)], [((16, rows), BF16)], "last_gram", *terms, estimates)
     terms = sum_over_row(gram)
     own = rows // lax.axis_size("col")
     piece = lax.dynamic_slice_in_dim(block, lax.axis_index("col") * own, own, 1)

time: 88.3 us -> 87.1 us (0.986)
  blocking collectives: 14.6 us -> 0 us
  starting transfers between devices: 36 us -> 42.7 us
  waiting for transfers between devices: 23.5 us -> 28.7 us
  Pallas kernels: 12.5 us -> 14.6 us
    all_to_all x1 -> x0, blocking collectives: 14.6 us -> none  [shards(): lax.all_to_all(copies, 'col', split_axis=0, concat_axis=0, tiled=True)]
    ppermute x24 -> x30, starting transfers between devices: 36 us -> 42.7 us  [exchange(): return lax.ppermute(value, axis, pairs)]
    ppermute x24 -> x30, waiting for transfers between devices: 23.5 us -> 28.7 us  [exchange(): return lax.ppermute(value, axis, pairs)]
    pallas_call x5 -> x6, Pallas kernels: 8.46 us -> 9.9 us  [call(): pl.pallas_call(kernel, out_shape=[jax.ShapeDtypeStruct(s, F32) for s in s...]
    pallas_call x1 -> x3, Pallas kernels: 4.01 us -> 4.74 us  [the longest x2 4.73 us: held_half(): pl.pallas_call(functools.partial(load_kernel, half * (rows // 2)), out_sh...]
  transfers between devices with their start and end apart: 24 -> 30, of which waited for: 20 -> 22; matrix products, arithmetic and copies ran while one was open for 0% -> 0% of each run, Pallas kernels for 0% -> 5%
where the time goes in v3:
time: 87.1 us; the launch traced here: 87 us
  starting transfers between devices  42.7 us (49%)
  waiting for transfers between devices  28.7 us (33%)
  Pallas kernels  14.6 us (17%)
    ppermute x30, starting transfers between devices, exchange(): return lax.ppermute(value, axis, pairs)  42.7 us
    ppermute x30, waiting for transfers between devices, exchange(): return lax.ppermute(value, axis, pairs)  28.7 us
    pallas_call x6, Pallas kernels, call(): pl.pallas_call(kernel, out_shape=[jax.ShapeDtypeStruct(s, F32) for s in s...  9.9 us
    pallas_call x2, Pallas kernels, held_half(): pl.pallas_call(functools.partial(load_kernel, half * (rows // 2)), out_sh...  4.73 us
  transfers between devices with their start and end apart: 30, of which 22 were waited for; matrix products, arithmetic and copies ran while one was open for 0% of the time, Pallas kernels for 5%

profile of v3, /device:TPU:0, one launch (start us, length us, event | category | flops | bytes accessed | tf_op | source)
XLA Modules:
  0.0 87.0 jit_solution(1895346299408881327)
XLA Ops:
  0.6 3.2 %collective-permute-start = (bf16[8,192]{1,0:T(8,128)(2,1)}, bf16[8,192]{1,0:T(8,128)(2,1)S(1)}, u32[]{:S(2)}, u32[]{:S(2)}) collective-permute-start(bf16[8,192]{1,0:T(8,128)(2,1)} %a_ref.1), channel_id=1, source_target_pairs={{0,2},{1,3},{2,0},{3,1},{4,6},{5,7},{6,4},{7,5},{8,10},{9,11},{10,... | collective-permute-start | bytes 9224 | tf_op jit(solution)/shard_map/ppermute | solution.py:21
  3.8 1.1 %collective-permute-start.1 = (bf16[8,192]{1,0:T(8,128)(2,1)}, bf16[8,192]{1,0:T(8,128)(2,1)S(1)}, u32[]{:S(2)}, u32[]{:S(2)}) collective-permute-start(bf16[8,192]{1,0:T(8,128)(2,1)} %a_ref.1), channel_id=1, source_target_pairs={{0,3},{1,0},{2,1},{3,2},{4,7},{5,4},{6,5},{7,6},{8,11},{9,8},{10,9... | collective-permute-start | bytes 9224 | tf_op jit(solution)/shard_map/ppermute | solution.py:21
  5.0 0.9 %collective-permute-start.2 = (bf16[8,192]{1,0:T(8,128)(2,1)}, bf16[8,192]{1,0:T(8,128)(2,1)S(1)}, u32[]{:S(2)}, u32[]{:S(2)}) collective-permute-start(bf16[8,192]{1,0:T(8,128)(2,1)} %a_ref.1), channel_id=1, source_target_pairs={{0,1},{1,2},{2,3},{3,0},{4,5},{5,6},{6,7},{7,4},{8,9},{9,10},{10,1... | collective-permute-start | bytes 9224 | tf_op jit(solution)/shard_map/ppermute | solution.py:21
  5.9 2.4 %held_half0.1.held_ref.refs_0_.refs_4_.refs_5_ = bf16[1536,1536]{1,0:T(8,128)(2,1)S(1)} custom-call(bf16[3072,1536]{1,0:T(8,128)(2,1)} %matrix_ref.3), custom_call_target="tpu_custom_call" | custom-call | bytes 4718592 | tf_op jit(solution)/shard_map/held_half0/pallas_call | solution.py:192
  8.2 1.7 %collective-permute-done.2.d_ref = bf16[8,192]{1,0:T(8,128)(2,1)S(1)} collective-permute-done((bf16[8,192]{1,0:T(8,128)(2,1)}, bf16[8,192]{1,0:T(8,128)(2,1)S(1)}, u32[]{:S(2)}, u32[]{:S(2)}) %collective-permute-start.2) | collective-permute-done | bytes 3104 | tf_op jit(solution)/shard_map/ppermute | solution.py:21
  10.0 3.2 %collective-permute-start.3 = (bf16[4,8,192]{2,1,0:T(8,128)(2,1)S(1)}, bf16[4,8,192]{2,1,0:T(8,128)(2,1)S(1)}, u32[]{:S(2)}, u32[]{:S(2)}) collective-permute-start(bf16[4,8,192]{2,1,0:T(8,128)(2,1)S(1)} %line.1.a_ref), channel_id=1, source_target_pairs={{0,8},{1,9},{2,10},{3,11},{4,12},{5,13},{6,14},{7,15},{8,0},{9,1},... | collective-permute-start | bytes 36872 | tf_op jit(solution)/shard_map/ppermute | solution.py:21
  13.2 1.1 %collective-permute-start.4 = (bf16[4,8,192]{2,1,0:T(8,128)(2,1)S(1)}, bf16[4,8,192]{2,1,0:T(8,128)(2,1)S(1)}, u32[]{:S(2)}, u32[]{:S(2)}) collective-permute-start(bf16[4,8,192]{2,1,0:T(8,128)(2,1)S(1)} %line.1.a_ref), channel_id=1, source_target_pairs={{0,12},{1,13},{2,14},{3,15},{4,0},{5,1},{6,2},{7,3},{8,4},{9,5},{1... | collective-permute-start | bytes 36872 | tf_op jit(solution)/shard_map/ppermute | solution.py:21
  14.3 1.0 %collective-permute-start.5 = (bf16[4,8,192]{2,1,0:T(8,128)(2,1)S(1)}, bf16[4,8,192]{2,1,0:T(8,128)(2,1)S(1)}, u32[]{:S(2)}, u32[]{:S(2)}) collective-permute-start(bf16[4,8,192]{2,1,0:T(8,128)(2,1)S(1)} %line.1.a_ref), channel_id=1, source_target_pairs={{0,4},{1,5},{2,6},{3,7},{4,8},{5,9},{6,10},{7,11},{8,12},{9,13},{1... | collective-permute-start | bytes 36872 | tf_op jit(solution)/shard_map/ppermute | solution.py:21
  15.2 2.4 %held_half1.1.refs_1_.refs_5_.refs_6_ = bf16[1536,1536]{1,0:T(8,128)(2,1)S(1)} custom-call(bf16[3072,1536]{1,0:T(8,128)(2,1)} %matrix_ref.3), custom_call_target="tpu_custom_call" | custom-call | bytes 4718592 | tf_op jit(solution)/shard_map/held_half1/pallas_call | solution.py:192
  17.6 1.6 %collective-permute-done.5.d_ref = bf16[4,8,192]{2,1,0:T(8,128)(2,1)S(1)} collective-permute-done((bf16[4,8,192]{2,1,0:T(8,128)(2,1)S(1)}, bf16[4,8,192]{2,1,0:T(8,128)(2,1)S(1)}, u32[]{:S(2)}, u32[]{:S(2)}) %collective-permute-start.5) | collective-permute-done | bytes 12320 | tf_op jit(solution)/shard_map/ppermute | solution.py:21
  19.2 1.4 %product1.1 = f32[8,1536]{1,0:T(8,128)S(1)} custom-call(bf16[4,8,192]{2,1,0:T(8,128)(2,1)S(1)} %line.1.a_ref, bf16[4,8,192]{2,1,0:T(8,128)(2,1)S(1)} %collective-permute-done.3.c_ref, bf16[4,8,192]{2,1,0:T(8,128)(2,1)S(1)} %collective-permute-done.4.b_ref, bf16[4,8,192]{2,1,0:T(8,128)(2,1)S(1)} %collective-permute-done.5.d_ref, ...), custom_call_target="tpu_custom_call" | custom-call | tf_op jit(solution)/shard_map/product1/pallas_call | solution.py:250
  20.6 1.2 %collective-permute-done.6 = f32[8,1536]{1,0:T(8,128)S(1)} collective-permute-done((f32[8,1536]{1,0:T(8,128)S(1)}, f32[8,1536]{1,0:T(8,128)S(1)}, u32[]{:S(2)}, u32[]{:S(2)}) %collective-permute-start.6) | collective-permute-done | bytes 49184 | tf_op jit(solution)/shard_map/ppermute | solution.py:21
  21.9 4.0 %collective-permute-start.7 = (f32[8,1536]{1,0:T(8,128)S(1)}, f32[8,1536]{1,0:T(8,128)S(1)}, u32[]{:S(2)}, u32[]{:S(2)}) collective-permute-start(f32[8,1536]{1,0:T(8,128)S(1)} %add.32.refs_0_), channel_id=1, source_target_pairs={{0,64},{16,80},{32,96},{48,112},{64,0},{80,16},{96,32},{112,48},{1... | collective-permute-start | bytes 147464 | tf_op jit(solution)/shard_map/ppermute | solution.py:21
  25.8 1.0 %collective-permute-start.8 = (f32[8,1536]{1,0:T(8,128)S(1)}, f32[8,1536]{1,0:T(8,128)S(1)}, u32[]{:S(2)}, u32[]{:S(2)}) collective-permute-start(f32[8,1536]{1,0:T(8,128)S(1)} %add.32.refs_0_), channel_id=1, source_target_pairs={{0,32},{16,48},{32,64},{48,80},{64,96},{80,112},{96,0},{112,16},{1... | collective-permute-start | bytes 147464 | tf_op jit(solution)/shard_map/ppermute | solution.py:21
  26.9 2.2 %collective-permute-start.9 = (f32[8,1536]{1,0:T(8,128)S(1)}, f32[8,1536]{1,0:T(8,128)S(1)}, u32[]{:S(2)}, u32[]{:S(2)}) collective-permute-start(f32[8,1536]{1,0:T(8,128)S(1)} %add.32.refs_0_), channel_id=1, source_target_pairs={{0,96},{16,112},{32,0},{48,16},{64,32},{80,48},{96,64},{112,80},{1... | collective-permute-start | bytes 147464 | tf_op jit(solution)/shard_map/ppermute | solution.py:21
  29.1 2.1 %collective-permute-done.8.refs_2_ = f32[8,1536]{1,0:T(8,128)S(1)} collective-permute-done((f32[8,1536]{1,0:T(8,128)S(1)}, f32[8,1536]{1,0:T(8,128)S(1)}, u32[]{:S(2)}, u32[]{:S(2)}) %collective-permute-start.8) | collective-permute-done | bytes 49184 | tf_op jit(solution)/shard_map/ppermute | solution.py:21
  31.2 2.9 %product2.1 = f32[8,3200]{1,0:T(8,128)S(1)} custom-call(f32[8,1536]{1,0:T(8,128)S(1)} %add.32.refs_0_, f32[8,1536]{1,0:T(8,128)S(1)} %collective-permute-done.7.refs_1_, f32[8,1536]{1,0:T(8,128)S(1)} %collective-permute-done.8.refs_2_, f32[8,1536]{1,0:T(8,128)S(1)} %collective-permute-done.9.refs_3_, ...), custom_call_target="tpu_custom_call" | custom-call | tf_op jit(solution)/shard_map/product2/pallas_call | solution.py:250
  34.5 1.3 %collective-permute-start.11 = (f32[8,3200]{1,0:T(8,128)S(1)}, f32[8,3200]{1,0:T(8,128)S(1)}, u32[]{:S(2)}, u32[]{:S(2)}) collective-permute-start(f32[8,3200]{1,0:T(8,128)S(1)} %product2.1), channel_id=1, source_target_pairs={{0,1},{1,2},{2,3},{3,0},{4,5},{5,6},{6,7},{7,4},{8,9},{9,10},{10,1... | collective-permute-start | bytes 307208 | tf_op jit(solution)/shard_map/ppermute | solution.py:21
  35.7 2.0 %collective-permute-start.12 = (f32[8,3200]{1,0:T(8,128)S(1)}, f32[8,3200]{1,0:T(8,128)S(1)}, u32[]{:S(2)}, u32[]{:S(2)}) collective-permute-start(f32[8,3200]{1,0:T(8,128)S(1)} %product2.1), channel_id=1, source_target_pairs={{0,3},{1,0},{2,1},{3,2},{4,7},{5,4},{6,5},{7,6},{8,11},{9,8},{10,9... | collective-permute-start | bytes 307208 | tf_op jit(solution)/shard_map/ppermute | solution.py:21
  37.7 2.7 %collective-permute-done.10 = f32[8,3200]{1,0:T(8,128)S(1)} collective-permute-done((f32[8,3200]{1,0:T(8,128)S(1)}, f32[8,3200]{1,0:T(8,128)S(1)}, u32[]{:S(2)}, u32[]{:S(2)}) %collective-permute-start.10) | collective-permute-done | bytes 102432 | tf_op jit(solution)/shard_map/ppermute | solution.py:21
  40.4 1.0 %collective-permute-done.11 = f32[8,3200]{1,0:T(8,128)S(1)} collective-permute-done((f32[8,3200]{1,0:T(8,128)S(1)}, f32[8,3200]{1,0:T(8,128)S(1)}, u32[]{:S(2)}, u32[]{:S(2)}) %collective-permute-start.11) | collective-permute-done | bytes 102432 | tf_op jit(solution)/shard_map/ppermute | solution.py:21
  42.0 1.1 %collective-permute-start.14 = (f32[8,3200]{1,0:T(8,128)S(1)}, f32[8,3200]{1,0:T(8,128)S(1)}, u32[]{:S(2)}, u32[]{:S(2)}) collective-permute-start(f32[8,3200]{1,0:T(8,128)S(1)} %add_add_fusion.1.refs_0_), channel_id=1, source_target_pairs={{0,4},{1,5},{2,6},{3,7},{4,8},{5,9},{6,10},{7,11},{8,12},{9,13},{1... | collective-permute-start | bytes 307208 | tf_op jit(solution)/shard_map/ppermute | solution.py:21
  43.1 2.1 %collective-permute-start.15 = (f32[8,3200]{1,0:T(8,128)S(1)}, f32[8,3200]{1,0:T(8,128)S(1)}, u32[]{:S(2)}, u32[]{:S(2)}) collective-permute-start(f32[8,3200]{1,0:T(8,128)S(1)} %add_add_fusion.1.refs_0_), channel_id=1, source_target_pairs={{0,12},{1,13},{2,14},{3,15},{4,0},{5,1},{6,2},{7,3},{8,4},{9,5},{1... | collective-permute-start | bytes 307208 | tf_op jit(solution)/shard_map/ppermute | solution.py:21
  45.2 2.6 %collective-permute-done.13.refs_1_ = f32[8,3200]{1,0:T(8,128)S(1)} collective-permute-done((f32[8,3200]{1,0:T(8,128)S(1)}, f32[8,3200]{1,0:T(8,128)S(1)}, u32[]{:S(2)}, u32[]{:S(2)}) %collective-permute-start.13) | collective-permute-done | bytes 102432 | tf_op jit(solution)/shard_map/ppermute | solution.py:21
  47.8 1.0 %collective-permute-done.14.refs_2_ = f32[8,3200]{1,0:T(8,128)S(1)} collective-permute-done((f32[8,3200]{1,0:T(8,128)S(1)}, f32[8,3200]{1,0:T(8,128)S(1)}, u32[]{:S(2)}, u32[]{:S(2)}) %collective-permute-start.14) | collective-permute-done | bytes 102432 | tf_op jit(solution)/shard_map/ppermute | solution.py:21
  48.8 1.6 %product3.1 = (f32[8,1664]{1,0:T(8,128)S(1)}, f32[8,128]{1,0:T(8,128)S(1)}) custom-call(f32[8,3200]{1,0:T(8,128)S(1)} %add_add_fusion.1.refs_0_, f32[8,3200]{1,0:T(8,128)S(1)} %collective-permute-done.13.refs_1_, f32[8,3200]{1,0:T(8,128)S(1)} %collective-permute-done.14.refs_2_, f32[8,3200]{1,0:T(8,128)S(1)} %collective-permute-done.15.refs_3_, ...), custom_call_target="tpu_custom_call" | custom-call | tf_op jit(solution)/shard_map/product3/pallas_call | solution.py:250
  50.5 1.2 %collective-permute-done.16 = f32[8,1664]{1,0:T(8,128)S(1)} collective-permute-done((f32[8,1664]{1,0:T(8,128)S(1)}, f32[8,1664]{1,0:T(8,128)S(1)}, u32[]{:S(2)}, u32[]{:S(2)}) %collective-permute-start.16) | collective-permute-done | bytes 53280 | tf_op jit(solution)/shard_map/ppermute | solution.py:21
  51.7 1.5 %collective-permute-start.17 = (f32[8,1664]{1,0:T(8,128)S(1)}, f32[8,1664]{1,0:T(8,128)S(1)}, u32[]{:S(2)}, u32[]{:S(2)}) collective-permute-start(f32[8,1664]{1,0:T(8,128)S(1)} %add.36.refs_0_), channel_id=1, source_target_pairs={{0,64},{16,80},{32,96},{48,112},{64,0},{80,16},{96,32},{112,48},{1... | collective-permute-start | bytes 159752 | tf_op jit(solution)/shard_map/ppermute | solution.py:21
  53.2 2.6 %collective-permute-start.18 = (f32[8,1664]{1,0:T(8,128)S(1)}, f32[8,1664]{1,0:T(8,128)S(1)}, u32[]{:S(2)}, u32[]{:S(2)}) collective-permute-start(f32[8,1664]{1,0:T(8,128)S(1)} %add.36.refs_0_), channel_id=1, source_target_pairs={{0,32},{16,48},{32,64},{48,80},{64,96},{80,112},{96,0},{112,16},{1... | collective-permute-start | bytes 159752 | tf_op jit(solution)/shard_map/ppermute | solution.py:21
  56.5 1.2 %collective-permute-done.17.refs_1_ = f32[8,1664]{1,0:T(8,128)S(1)} collective-permute-done((f32[8,1664]{1,0:T(8,128)S(1)}, f32[8,1664]{1,0:T(8,128)S(1)}, u32[]{:S(2)}, u32[]{:S(2)}) %collective-permute-start.17) | collective-permute-done | bytes 53280 | tf_op jit(solution)/shard_map/ppermute | solution.py:21
  57.7 0.9 %collective-permute-done.18.refs_2_ = f32[8,1664]{1,0:T(8,128)S(1)} collective-permute-done((f32[8,1664]{1,0:T(8,128)S(1)}, f32[8,1664]{1,0:T(8,128)S(1)}, u32[]{:S(2)}, u32[]{:S(2)}) %collective-permute-start.18) | collective-permute-done | bytes 53280 | tf_op jit(solution)/shard_map/ppermute | solution.py:21
  58.6 1.4 %collective-permute-done.19.refs_3_ = f32[8,1664]{1,0:T(8,128)S(1)} collective-permute-done((f32[8,1664]{1,0:T(8,128)S(1)}, f32[8,1664]{1,0:T(8,128)S(1)}, u32[]{:S(2)}, u32[]{:S(2)}) %collective-permute-start.19) | collective-permute-done | bytes 53280 | tf_op jit(solution)/shard_map/ppermute | solution.py:21
  60.0 2.7 %product4.1 = (f32[8,3200]{1,0:T(8,128)S(1)}, f32[8,128]{1,0:T(8,128)S(1)}) custom-call(f32[8,1664]{1,0:T(8,128)S(1)} %add.36.refs_0_, f32[8,1664]{1,0:T(8,128)S(1)} %collective-permute-done.17.refs_1_, f32[8,1664]{1,0:T(8,128)S(1)} %collective-permute-done.18.refs_2_, f32[8,1664]{1,0:T(8,128)S(1)} %collective-permute-done.19.refs_3_, ...), custom_call_target="tpu_custom_call" | custom-call | tf_op jit(solution)/shard_map/product4/pallas_call | solution.py:250
  62.7 1.2 %collective-permute-start.20 = (f32[8,3200]{1,0:T(8,128)S(1)}, f32[8,3200]{1,0:T(8,128)S(1)}, u32[]{:S(2)}, u32[]{:S(2)}) collective-permute-start(f32[8,3200]{1,0:T(8,128)S(1)} %get-tuple-element.13), channel_id=1, source_target_pairs={{0,2},{1,3},{2,0},{3,1},{4,6},{5,7},{6,4},{7,5},{8,10},{9,11},{10,... | collective-permute-start | bytes 307208 | tf_op jit(solution)/shard_map/ppermute | solution.py:21
  64.0 1.8 %collective-permute-start.21 = (f32[8,3200]{1,0:T(8,128)S(1)}, f32[8,3200]{1,0:T(8,128)S(1)}, u32[]{:S(2)}, u32[]{:S(2)}) collective-permute-start(f32[8,3200]{1,0:T(8,128)S(1)} %get-tuple-element.13), channel_id=1, source_target_pairs={{0,1},{1,2},{2,3},{3,0},{4,5},{5,6},{6,7},{7,4},{8,9},{9,10},{10,1... | collective-permute-start | bytes 307208 | tf_op jit(solution)/shard_map/ppermute | solution.py:21
  65.8 1.4 %collective-permute-start.22 = (f32[8,3200]{1,0:T(8,128)S(1)}, f32[8,3200]{1,0:T(8,128)S(1)}, u32[]{:S(2)}, u32[]{:S(2)}) collective-permute-start(f32[8,3200]{1,0:T(8,128)S(1)} %get-tuple-element.13), channel_id=1, source_target_pairs={{0,3},{1,0},{2,1},{3,2},{4,7},{5,4},{6,5},{7,6},{8,11},{9,8},{10,9... | collective-permute-start | bytes 307208 | tf_op jit(solution)/shard_map/ppermute | solution.py:21
  67.2 1.8 %collective-permute-done.20 = f32[8,3200]{1,0:T(8,128)S(1)} collective-permute-done((f32[8,3200]{1,0:T(8,128)S(1)}, f32[8,3200]{1,0:T(8,128)S(1)}, u32[]{:S(2)}, u32[]{:S(2)}) %collective-permute-start.20) | collective-permute-done | bytes 102432 | tf_op jit(solution)/shard_map/ppermute | solution.py:21
  69.0 1.1 %collective-permute-done.21 = f32[8,3200]{1,0:T(8,128)S(1)} collective-permute-done((f32[8,3200]{1,0:T(8,128)S(1)}, f32[8,3200]{1,0:T(8,128)S(1)}, u32[]{:S(2)}, u32[]{:S(2)}) %collective-permute-start.21) | collective-permute-done | bytes 102432 | tf_op jit(solution)/shard_map/ppermute | solution.py:21
  70.5 1.3 %collective-permute-start.23 = (f32[8,3200]{1,0:T(8,128)S(1)}, f32[8,3200]{1,0:T(8,128)S(1)}, u32[]{:S(2)}, u32[]{:S(2)}) collective-permute-start(f32[8,3200]{1,0:T(8,128)S(1)} %add_add_fusion.refs_0_), channel_id=1, source_target_pairs={{0,8},{1,9},{2,10},{3,11},{4,12},{5,13},{6,14},{7,15},{8,0},{9,1},... | collective-permute-start | bytes 307208 | tf_op jit(solution)/shard_map/ppermute | solution.py:21
  71.8 1.9 %collective-permute-start.24 = (f32[8,3200]{1,0:T(8,128)S(1)}, f32[8,3200]{1,0:T(8,128)S(1)}, u32[]{:S(2)}, u32[]{:S(2)}) collective-permute-start(f32[8,3200]{1,0:T(8,128)S(1)} %add_add_fusion.refs_0_), channel_id=1, source_target_pairs={{0,4},{1,5},{2,6},{3,7},{4,8},{5,9},{6,10},{7,11},{8,12},{9,13},{1... | collective-permute-start | bytes 307208 | tf_op jit(solution)/shard_map/ppermute | solution.py:21
  73.7 1.4 %collective-permute-start.25 = (f32[8,3200]{1,0:T(8,128)S(1)}, f32[8,3200]{1,0:T(8,128)S(1)}, u32[]{:S(2)}, u32[]{:S(2)}) collective-permute-start(f32[8,3200]{1,0:T(8,128)S(1)} %add_add_fusion.refs_0_), channel_id=1, source_target_pairs={{0,12},{1,13},{2,14},{3,15},{4,0},{5,1},{6,2},{7,3},{8,4},{9,5},{1... | collective-permute-start | bytes 307208 | tf_op jit(solution)/shard_map/ppermute | solution.py:21
  75.0 1.7 %collective-permute-done.23.refs_1_ = f32[8,3200]{1,0:T(8,128)S(1)} collective-permute-done((f32[8,3200]{1,0:T(8,128)S(1)}, f32[8,3200]{1,0:T(8,128)S(1)}, u32[]{:S(2)}, u32[]{:S(2)}) %collective-permute-start.23) | collective-permute-done | bytes 102432 | tf_op jit(solution)/shard_map/ppermute | solution.py:21
  76.7 1.1 %collective-permute-done.24.refs_2_ = f32[8,3200]{1,0:T(8,128)S(1)} collective-permute-done((f32[8,3200]{1,0:T(8,128)S(1)}, f32[8,3200]{1,0:T(8,128)S(1)}, u32[]{:S(2)}, u32[]{:S(2)}) %collective-permute-start.24) | collective-permute-done | bytes 102432 | tf_op jit(solution)/shard_map/ppermute | solution.py:21
  78.8 1.2 %collective-permute-done.26 = f32[8,128]{1,0:T(8,128)S(1)} collective-permute-done((f32[8,128]{1,0:T(8,128)S(1)}, f32[8,128]{1,0:T(8,128)S(1)}, u32[]{:S(2)}, u32[]{:S(2)}) %collective-permute-start.26) | collective-permute-done | bytes 4128 | tf_op jit(solution)/shard_map/ppermute | solution.py:21
  80.6 2.0 %collective-permute-start.28 = (f32[8,128]{1,0:T(8,128)S(1)}, f32[8,128]{1,0:T(8,128)S(1)}, u32[]{:S(2)}, u32[]{:S(2)}) collective-permute-start(f32[8,128]{1,0:T(8,128)S(1)} %add.40.a_ref), channel_id=1, source_target_pairs={{0,32},{16,48},{32,64},{48,80},{64,96},{80,112},{96,0},{112,16},{1... | collective-permute-start | bytes 12296 | tf_op jit(solution)/shard_map/ppermute | solution.py:21
  82.6 1.2 %collective-permute-start.29 = (f32[8,128]{1,0:T(8,128)S(1)}, f32[8,128]{1,0:T(8,128)S(1)}, u32[]{:S(2)}, u32[]{:S(2)}) collective-permute-start(f32[8,128]{1,0:T(8,128)S(1)} %add.40.a_ref), channel_id=1, source_target_pairs={{0,96},{16,112},{32,0},{48,16},{64,32},{80,48},{96,64},{112,80},{1... | collective-permute-start | bytes 12296 | tf_op jit(solution)/shard_map/ppermute | solution.py:21
  83.9 1.1 %collective-permute-done.27.b_ref = f32[8,128]{1,0:T(8,128)S(1)} collective-permute-done((f32[8,128]{1,0:T(8,128)S(1)}, f32[8,128]{1,0:T(8,128)S(1)}, u32[]{:S(2)}, u32[]{:S(2)}) %collective-permute-start.27) | collective-permute-done | bytes 4128 | tf_op jit(solution)/shard_map/ppermute | solution.py:21
  85.4 0.8 collective-permute-done.29.d_ref
  (31 shorter events, 4.8 us)
Async XLA Ops:
  0.6 9.4 %copy-start = (bf16[8,192]{1,0:T(8,128)(2,1)S(1)}, bf16[8,192]{1,0:T(8,128)(2,1)}, u32[]{:S(2)}) copy-start(bf16[8,192]{1,0:T(8,128)(2,1)} %a_ref.1) | copy-start | bytes 9220
  0.6 7.6 %collective-permute-start = (bf16[8,192]{1,0:T(8,128)(2,1)}, bf16[8,192]{1,0:T(8,128)(2,1)S(1)}, u32[]{:S(2)}, u32[]{:S(2)}) collective-permute-start(bf16[8,192]{1,0:T(8,128)(2,1)} %a_ref.1), channel_id=1, source_target_pairs={{0,2},{1,3},{2,0},{3,1},{4,6},{5,7},{6,4},{7,5},{8,10},{9,11},{10,... | collective-permute-start | bytes 9224 | tf_op jit(solution)/shard_map/ppermute | solution.py:21
  3.8 4.4 %collective-permute-start.1 = (bf16[8,192]{1,0:T(8,128)(2,1)}, bf16[8,192]{1,0:T(8,128)(2,1)S(1)}, u32[]{:S(2)}, u32[]{:S(2)}) collective-permute-start(bf16[8,192]{1,0:T(8,128)(2,1)} %a_ref.1), channel_id=1, source_target_pairs={{0,3},{1,0},{2,1},{3,2},{4,7},{5,4},{6,5},{7,6},{8,11},{9,8},{10,9... | collective-permute-start | bytes 9224 | tf_op jit(solution)/shard_map/ppermute | solution.py:21
  5.0 5.0 %collective-permute-start.2 = (bf16[8,192]{1,0:T(8,128)(2,1)}, bf16[8,192]{1,0:T(8,128)(2,1)S(1)}, u32[]{:S(2)}, u32[]{:S(2)}) collective-permute-start(bf16[8,192]{1,0:T(8,128)(2,1)} %a_ref.1), channel_id=1, source_target_pairs={{0,1},{1,2},{2,3},{3,0},{4,5},{5,6},{6,7},{7,4},{8,9},{9,10},{10,1... | collective-permute-start | bytes 9224 | tf_op jit(solution)/shard_map/ppermute | solution.py:21
  10.0 7.6 %collective-permute-start.3 = (bf16[4,8,192]{2,1,0:T(8,128)(2,1)S(1)}, bf16[4,8,192]{2,1,0:T(8,128)(2,1)S(1)}, u32[]{:S(2)}, u32[]{:S(2)}) collective-permute-start(bf16[4,8,192]{2,1,0:T(8,128)(2,1)S(1)} %line.1.a_ref), channel_id=1, source_target_pairs={{0,8},{1,9},{2,10},{3,11},{4,12},{5,13},{6,14},{7,15},{8,0},{9,1},... | collective-permute-start | bytes 36872 | tf_op jit(solution)/shard_map/ppermute | solution.py:21
  13.2 4.4 %collective-permute-start.4 = (bf16[4,8,192]{2,1,0:T(8,128)(2,1)S(1)}, bf16[4,8,192]{2,1,0:T(8,128)(2,1)S(1)}, u32[]{:S(2)}, u32[]{:S(2)}) collective-permute-start(bf16[4,8,192]{2,1,0:T(8,128)(2,1)S(1)} %line.1.a_ref), channel_id=1, source_target_pairs={{0,12},{1,13},{2,14},{3,15},{4,0},{5,1},{6,2},{7,3},{8,4},{9,5},{1... | collective-permute-start | bytes 36872 | tf_op jit(solution)/shard_map/ppermute | solution.py:21
  14.3 4.9 %collective-permute-start.5 = (bf16[4,8,192]{2,1,0:T(8,128)(2,1)S(1)}, bf16[4,8,192]{2,1,0:T(8,128)(2,1)S(1)}, u32[]{:S(2)}, u32[]{:S(2)}) collective-permute-start(bf16[4,8,192]{2,1,0:T(8,128)(2,1)S(1)} %line.1.a_ref), channel_id=1, source_target_pairs={{0,4},{1,5},{2,6},{3,7},{4,8},{5,9},{6,10},{7,11},{8,12},{9,13},{1... | collective-permute-start | bytes 36872 | tf_op jit(solution)/shard_map/ppermute | solution.py:21
  20.6 1.2 %collective-permute-start.6 = (f32[8,1536]{1,0:T(8,128)S(1)}, f32[8,1536]{1,0:T(8,128)S(1)}, u32[]{:S(2)}, u32[]{:S(2)}) collective-permute-start(f32[8,1536]{1,0:T(8,128)S(1)} %product1.1), channel_id=1, source_target_pairs={{0,16},{16,0},{32,48},{48,32},{64,80},{80,64},{96,112},{112,96},{1... | collective-permute-start | bytes 147464 | tf_op jit(solution)/shard_map/ppermute | solution.py:21
  21.9 7.2 %collective-permute-start.7 = (f32[8,1536]{1,0:T(8,128)S(1)}, f32[8,1536]{1,0:T(8,128)S(1)}, u32[]{:S(2)}, u32[]{:S(2)}) collective-permute-start(f32[8,1536]{1,0:T(8,128)S(1)} %add.32.refs_0_), channel_id=1, source_target_pairs={{0,64},{16,80},{32,96},{48,112},{64,0},{80,16},{96,32},{112,48},{1... | collective-permute-start | bytes 147464 | tf_op jit(solution)/shard_map/ppermute | solution.py:21
  25.8 5.3 %collective-permute-start.8 = (f32[8,1536]{1,0:T(8,128)S(1)}, f32[8,1536]{1,0:T(8,128)S(1)}, u32[]{:S(2)}, u32[]{:S(2)}) collective-permute-start(f32[8,1536]{1,0:T(8,128)S(1)} %add.32.refs_0_), channel_id=1, source_target_pairs={{0,32},{16,48},{32,64},{48,80},{64,96},{80,112},{96,0},{112,16},{1... | collective-permute-start | bytes 147464 | tf_op jit(solution)/shard_map/ppermute | solution.py:21
  26.9 4.3 %collective-permute-start.9 = (f32[8,1536]{1,0:T(8,128)S(1)}, f32[8,1536]{1,0:T(8,128)S(1)}, u32[]{:S(2)}, u32[]{:S(2)}) collective-permute-start(f32[8,1536]{1,0:T(8,128)S(1)} %add.32.refs_0_), channel_id=1, source_target_pairs={{0,96},{16,112},{32,0},{48,16},{64,32},{80,48},{96,64},{112,80},{1... | collective-permute-start | bytes 147464 | tf_op jit(solution)/shard_map/ppermute | solution.py:21
  34.1 6.3 %collective-permute-start.10 = (f32[8,3200]{1,0:T(8,128)S(1)}, f32[8,3200]{1,0:T(8,128)S(1)}, u32[]{:S(2)}, u32[]{:S(2)}) collective-permute-start(f32[8,3200]{1,0:T(8,128)S(1)} %product2.1), channel_id=1, source_target_pairs={{0,2},{1,3},{2,0},{3,1},{4,6},{5,7},{6,4},{7,5},{8,10},{9,11},{10,... | collective-permute-start | bytes 307208 | tf_op jit(solution)/shard_map/ppermute | solution.py:21
  34.5 7.0 %collective-permute-start.11 = (f32[8,3200]{1,0:T(8,128)S(1)}, f32[8,3200]{1,0:T(8,128)S(1)}, u32[]{:S(2)}, u32[]{:S(2)}) collective-permute-start(f32[8,3200]{1,0:T(8,128)S(1)} %product2.1), channel_id=1, source_target_pairs={{0,1},{1,2},{2,3},{3,0},{4,5},{5,6},{6,7},{7,4},{8,9},{9,10},{10,1... | collective-permute-start | bytes 307208 | tf_op jit(solution)/shard_map/ppermute | solution.py:21
  35.7 5.7 %collective-permute-start.12 = (f32[8,3200]{1,0:T(8,128)S(1)}, f32[8,3200]{1,0:T(8,128)S(1)}, u32[]{:S(2)}, u32[]{:S(2)}) collective-permute-start(f32[8,3200]{1,0:T(8,128)S(1)} %product2.1), channel_id=1, source_target_pairs={{0,3},{1,0},{2,1},{3,2},{4,7},{5,4},{6,5},{7,6},{8,11},{9,8},{10,9... | collective-permute-start | bytes 307208 | tf_op jit(solution)/shard_map/ppermute | solution.py:21
  41.5 6.3 %collective-permute-start.13 = (f32[8,3200]{1,0:T(8,128)S(1)}, f32[8,3200]{1,0:T(8,128)S(1)}, u32[]{:S(2)}, u32[]{:S(2)}) collective-permute-start(f32[8,3200]{1,0:T(8,128)S(1)} %add_add_fusion.1.refs_0_), channel_id=1, source_target_pairs={{0,8},{1,9},{2,10},{3,11},{4,12},{5,13},{6,14},{7,15},{8,0},{9,1},... | collective-permute-start | bytes 307208 | tf_op jit(solution)/shard_map/ppermute | solution.py:21
  42.0 6.8 %collective-permute-start.14 = (f32[8,3200]{1,0:T(8,128)S(1)}, f32[8,3200]{1,0:T(8,128)S(1)}, u32[]{:S(2)}, u32[]{:S(2)}) collective-permute-start(f32[8,3200]{1,0:T(8,128)S(1)} %add_add_fusion.1.refs_0_), channel_id=1, source_target_pairs={{0,4},{1,5},{2,6},{3,7},{4,8},{5,9},{6,10},{7,11},{8,12},{9,13},{1... | collective-permute-start | bytes 307208 | tf_op jit(solution)/shard_map/ppermute | solution.py:21
  43.1 5.7 %collective-permute-start.15 = (f32[8,3200]{1,0:T(8,128)S(1)}, f32[8,3200]{1,0:T(8,128)S(1)}, u32[]{:S(2)}, u32[]{:S(2)}) collective-permute-start(f32[8,3200]{1,0:T(8,128)S(1)} %add_add_fusion.1.refs_0_), channel_id=1, source_target_pairs={{0,12},{1,13},{2,14},{3,15},{4,0},{5,1},{6,2},{7,3},{8,4},{9,5},{1... | collective-permute-start | bytes 307208 | tf_op jit(solution)/shard_map/ppermute | solution.py:21
  50.4 1.2 %collective-permute-start.16 = (f32[8,1664]{1,0:T(8,128)S(1)}, f32[8,1664]{1,0:T(8,128)S(1)}, u32[]{:S(2)}, u32[]{:S(2)}) collective-permute-start(f32[8,1664]{1,0:T(8,128)S(1)} %get-tuple-element.11), channel_id=1, source_target_pairs={{0,16},{16,0},{32,48},{48,32},{64,80},{80,64},{96,112},{112,96},{1... | collective-permute-start | bytes 159752 | tf_op jit(solution)/shard_map/ppermute | solution.py:21
  51.7 6.0 %collective-permute-start.17 = (f32[8,1664]{1,0:T(8,128)S(1)}, f32[8,1664]{1,0:T(8,128)S(1)}, u32[]{:S(2)}, u32[]{:S(2)}) collective-permute-start(f32[8,1664]{1,0:T(8,128)S(1)} %add.36.refs_0_), channel_id=1, source_target_pairs={{0,64},{16,80},{32,96},{48,112},{64,0},{80,16},{96,32},{112,48},{1... | collective-permute-start | bytes 159752 | tf_op jit(solution)/shard_map/ppermute | solution.py:21
  53.2 5.3 %collective-permute-start.18 = (f32[8,1664]{1,0:T(8,128)S(1)}, f32[8,1664]{1,0:T(8,128)S(1)}, u32[]{:S(2)}, u32[]{:S(2)}) collective-permute-start(f32[8,1664]{1,0:T(8,128)S(1)} %add.36.refs_0_), channel_id=1, source_target_pairs={{0,32},{16,48},{32,64},{48,80},{64,96},{80,112},{96,0},{112,16},{1... | collective-permute-start | bytes 159752 | tf_op jit(solution)/shard_map/ppermute | solution.py:21
  55.9 4.1 %collective-permute-start.19 = (f32[8,1664]{1,0:T(8,128)S(1)}, f32[8,1664]{1,0:T(8,128)S(1)}, u32[]{:S(2)}, u32[]{:S(2)}) collective-permute-start(f32[8,1664]{1,0:T(8,128)S(1)} %add.36.refs_0_), channel_id=1, source_target_pairs={{0,96},{16,112},{32,0},{48,16},{64,32},{80,48},{96,64},{112,80},{1... | collective-permute-start | bytes 159752 | tf_op jit(solution)/shard_map/ppermute | solution.py:21
  62.7 6.2 %collective-permute-start.20 = (f32[8,3200]{1,0:T(8,128)S(1)}, f32[8,3200]{1,0:T(8,128)S(1)}, u32[]{:S(2)}, u32[]{:S(2)}) collective-permute-start(f32[8,3200]{1,0:T(8,128)S(1)} %get-tuple-element.13), channel_id=1, source_target_pairs={{0,2},{1,3},{2,0},{3,1},{4,6},{5,7},{6,4},{7,5},{8,10},{9,11},{10,... | collective-permute-start | bytes 307208 | tf_op jit(solution)/shard_map/ppermute | solution.py:21
  64.0 6.1 %collective-permute-start.21 = (f32[8,3200]{1,0:T(8,128)S(1)}, f32[8,3200]{1,0:T(8,128)S(1)}, u32[]{:S(2)}, u32[]{:S(2)}) collective-permute-start(f32[8,3200]{1,0:T(8,128)S(1)} %get-tuple-element.13), channel_id=1, source_target_pairs={{0,1},{1,2},{2,3},{3,0},{4,5},{5,6},{6,7},{7,4},{8,9},{9,10},{10,1... | collective-permute-start | bytes 307208 | tf_op jit(solution)/shard_map/ppermute | solution.py:21
  65.8 4.7 %collective-permute-start.22 = (f32[8,3200]{1,0:T(8,128)S(1)}, f32[8,3200]{1,0:T(8,128)S(1)}, u32[]{:S(2)}, u32[]{:S(2)}) collective-permute-start(f32[8,3200]{1,0:T(8,128)S(1)} %get-tuple-element.13), channel_id=1, source_target_pairs={{0,3},{1,0},{2,1},{3,2},{4,7},{5,4},{6,5},{7,6},{8,11},{9,8},{10,9... | collective-permute-start | bytes 307208 | tf_op jit(solution)/shard_map/ppermute | solution.py:21
  70.5 6.3 %collective-permute-start.23 = (f32[8,3200]{1,0:T(8,128)S(1)}, f32[8,3200]{1,0:T(8,128)S(1)}, u32[]{:S(2)}, u32[]{:S(2)}) collective-permute-start(f32[8,3200]{1,0:T(8,128)S(1)} %add_add_fusion.refs_0_), channel_id=1, source_target_pairs={{0,8},{1,9},{2,10},{3,11},{4,12},{5,13},{6,14},{7,15},{8,0},{9,1},... | collective-permute-start | bytes 307208 | tf_op jit(solution)/shard_map/ppermute | solution.py:21
  71.8 6.0 %collective-permute-start.24 = (f32[8,3200]{1,0:T(8,128)S(1)}, f32[8,3200]{1,0:T(8,128)S(1)}, u32[]{:S(2)}, u32[]{:S(2)}) collective-permute-start(f32[8,3200]{1,0:T(8,128)S(1)} %add_add_fusion.refs_0_), channel_id=1, source_target_pairs={{0,4},{1,5},{2,6},{3,7},{4,8},{5,9},{6,10},{7,11},{8,12},{9,13},{1... | collective-permute-start | bytes 307208 | tf_op jit(solution)/shard_map/ppermute | solution.py:21
  73.7 4.7 %collective-permute-start.25 = (f32[8,3200]{1,0:T(8,128)S(1)}, f32[8,3200]{1,0:T(8,128)S(1)}, u32[]{:S(2)}, u32[]{:S(2)}) collective-permute-start(f32[8,3200]{1,0:T(8,128)S(1)} %add_add_fusion.refs_0_), channel_id=1, source_target_pairs={{0,12},{1,13},{2,14},{3,15},{4,0},{5,1},{6,2},{7,3},{8,4},{9,5},{1... | collective-permute-start | bytes 307208 | tf_op jit(solution)/shard_map/ppermute | solution.py:21
  78.7 1.2 %collective-permute-start.26 = (f32[8,128]{1,0:T(8,128)S(1)}, f32[8,128]{1,0:T(8,128)S(1)}, u32[]{:S(2)}, u32[]{:S(2)}) collective-permute-start(f32[8,128]{1,0:T(8,128)S(1)} %get-tuple-element.15), channel_id=1, source_target_pairs={{0,16},{16,0},{32,48},{48,32},{64,80},{80,64},{96,112},{112,96},{1... | collective-permute-start | bytes 12296 | tf_op jit(solution)/shard_map/ppermute | solution.py:21
  79.9 5.1 %collective-permute-start.27 = (f32[8,128]{1,0:T(8,128)S(1)}, f32[8,128]{1,0:T(8,128)S(1)}, u32[]{:S(2)}, u32[]{:S(2)}) collective-permute-start(f32[8,128]{1,0:T(8,128)S(1)} %add.40.a_ref), channel_id=1, source_target_pairs={{0,64},{16,80},{32,96},{48,112},{64,0},{80,16},{96,32},{112,48},{1... | collective-permute-start | bytes 12296 | tf_op jit(solution)/shard_map/ppermute | solution.py:21
  80.6 4.8 %collective-permute-start.28 = (f32[8,128]{1,0:T(8,128)S(1)}, f32[8,128]{1,0:T(8,128)S(1)}, u32[]{:S(2)}, u32[]{:S(2)}) collective-permute-start(f32[8,128]{1,0:T(8,128)S(1)} %add.40.a_ref), channel_id=1, source_target_pairs={{0,32},{16,48},{32,64},{48,80},{64,96},{80,112},{96,0},{112,16},{1... | collective-permute-start | bytes 12296 | tf_op jit(solution)/shard_map/ppermute | solution.py:21
  82.6 3.6 %collective-permute-start.29 = (f32[8,128]{1,0:T(8,128)S(1)}, f32[8,128]{1,0:T(8,128)S(1)}, u32[]{:S(2)}, u32[]{:S(2)}) collective-permute-start(f32[8,128]{1,0:T(8,128)S(1)} %add.40.a_ref), channel_id=1, source_target_pairs={{0,96},{16,112},{32,0},{48,16},{64,32},{80,48},{96,64},{112,80},{1... | collective-permute-start | bytes 12296 | tf_op jit(solution)/shard_map/ppermute | solution.py:21
